TPU v7x, 256 devices: a whole 4x4x8 slice. The times are simulated.
256 devices in a mesh: cols: 32 (over y, z), mem: 8 (over x, core).
Axes of the slice: x: 4, y: 4, z: 8, core: 2. Of those that a mesh axis runs over, the one named last changes fastest.
Arguments:
- state: float32 [80, 1048576], P('mem', 'cols'), may hold values from -6 to 6
- obs_value: float32 [4, 1024], P(None, 'cols'), may hold values from -6 to 6
- obs_var: float32 [4, 1024], P(None, 'cols'), may hold values from 0.2 to 2
- owner: int32 [4, 1024, 1], P(None, 'cols'), may hold values from 0 to 31; in each aligned block of 32 rows (0 to 31, 32 to 63, ..., all dimensions but the last counted through in order) at most 2 rows name the same one
- tile_of: int32 [4, 1024], P(None, 'cols'), may hold values from 0 to 63
- offsets: int32 [4, 1024, 4], P(None, 'cols'), may hold values from 0 to 511
- accept: int32 [4, 1024], P(None, 'cols'), may hold values 0 or 1
- loc_mask: int32 [2048, 4, 8], P(('cols', 'mem')), may hold values 0 or 1
Outputs:
- posterior: float32 [80, 1048576], P(None, ('cols', 'mem'))
Inputs may be any that keep to these rules, and one draw needn't show every extreme that they name: Within the 32 observations of one batch held by one index of cols, no owner is named more than 2 times, and that many is reached.
All inputs are finite; a program needn't handle non-finite values. No bound on the sum of `accept` or of `loc_mask` on one device may be relied on, other than what follows from the above.
Results may differ from a plain program's by a relative error of at most 0.0002.
Values sent between devices are 32-bit elements; how exact they have to be, the bound alone decides.
A program may use at most 64 MiB of HBM per device.

v0:
```python
import jax
import jax.numpy as jnp
from jax import lax
from jax.sharding import PartitionSpec as P

epsilon = 1e-05
EXACT = lax.Precision.HIGHEST


def innovations(prior_obs, observed, obs_noise, accepted):
    members = prior_obs.shape[0]
    mean_prior = jnp.mean(prior_obs, axis=0)
    spread = prior_obs - mean_prior
    spread_var = jnp.sum(spread * spread, axis=0) / (members - 1) + epsilon
    denominator = spread_var + obs_noise
    mean_shift = spread_var / denominator * (observed - mean_prior)
    factor = jnp.sqrt(obs_noise / denominator) - 1.0
    increment = accepted * (mean_shift + factor * spread)
    scaled = spread / ((members - 1) * spread_var)
    return (increment, scaled)


def local(state, obs_value, obs_var, owner, tile_of, offsets, accept, loc_mask):
    col_devices = lax.axis_size("cols")
    mem_devices = lax.axis_size("mem")
    source = lax.axis_index("cols")
    mem_index = lax.axis_index("mem")
    batch_total, per_src = obs_value.shape
    pick_count = offsets.shape[2]
    members = state.shape[0] * mem_devices
    cell_count = state.shape[1] // mem_devices
    tiles_here = loc_mask.shape[0]
    tile_len = cell_count // tiles_here
    block_count = loc_mask.shape[2]
    batch_obs = per_src * col_devices
    block_len = batch_obs // block_count
    capacity = max(2, 2 * per_src // col_devices)
    slot_count = col_devices * capacity
    destination = owner[:, :, 0]
    ordinal = jnp.arange(per_src, dtype=jnp.int32)
    same_owner = destination[:, :, None] == destination[:, None, :]
    earlier = (ordinal[None, :] < ordinal[:, None])[None]
    slot_rank = jnp.sum((same_owner & earlier).astype(jnp.int32), axis=2)
    batch_rows = jnp.broadcast_to(
        jnp.arange(batch_total, dtype=jnp.int32)[:, None], destination.shape
    )
    position = jnp.broadcast_to(source * per_src + ordinal, destination.shape)
    fields = jnp.concatenate(
        [tile_of[:, :, None], accept[:, :, None], position[:, :, None], offsets], axis=2
    )
    blank_int = (
        jnp.zeros((batch_total, col_devices, capacity, 3 + pick_count), jnp.int32)
        .at[:, :, :, 2]
        .set(-1)
    )
    sent_int = blank_int.at[batch_rows, destination, slot_rank].set(fields)
    blank_val = (
        jnp.zeros((batch_total, col_devices, capacity, 2), jnp.float32).at[:, :, :, 1].set(1.0)
    )
    sent_val = blank_val.at[batch_rows, destination, slot_rank].set(
        jnp.stack([obs_value, obs_var], axis=2)
    )
    arrived_int = lax.all_to_all(sent_int, "cols", split_axis=1, concat_axis=1, tiled=True).reshape(
        batch_total, slot_count, 3 + pick_count
    )
    arrived_val = lax.all_to_all(sent_val, "cols", split_axis=1, concat_axis=1, tiled=True).reshape(
        batch_total, slot_count, 2
    )
    obs_tile = arrived_int[:, :, 0]
    obs_flag = arrived_int[:, :, 1].astype(jnp.float32)
    obs_pos = arrived_int[:, :, 2]
    obs_off = arrived_int[:, :, 3:]
    observed = arrived_val[:, :, 0]
    obs_noise = arrived_val[:, :, 1]
    targets = jnp.where(obs_pos >= 0, obs_pos, batch_obs)
    ensemble = lax.all_to_all(state, "mem", split_axis=1, concat_axis=0, tiled=True)
    for batch_no in range(batch_total):
        local_cell = (
            obs_tile[batch_no][:, None] * tile_len + obs_off[batch_no] - mem_index * cell_count
        )
        inside = (local_cell >= 0) & (local_cell < cell_count) & (obs_pos[batch_no] >= 0)[:, None]
        flat_cells = jnp.clip(local_cell, 0, cell_count - 1).reshape(-1)
        picked = jnp.take(ensemble, flat_cells, axis=1).reshape(members, slot_count, pick_count)
        prior_obs = lax.psum(
            jnp.sum(jnp.where(inside[None], picked, 0.0), axis=2) / pick_count, "mem"
        )
        increment, scaled = innovations(
            prior_obs, observed[batch_no], obs_noise[batch_no], obs_flag[batch_no]
        )
        blank_panel = jnp.zeros((members, batch_obs), jnp.float32)
        placed_inc = blank_panel.at[:, targets[batch_no]].add(increment, mode="drop")
        placed_scl = blank_panel.at[:, targets[batch_no]].add(scaled, mode="drop")
        inc_all, scl_all = lax.psum((placed_inc, placed_scl), "cols")
        mask_now = loc_mask[:, batch_no, :].astype(jnp.float32)
        mean_state = jnp.mean(ensemble, axis=0)
        deviation = (ensemble - mean_state).reshape(members, tiles_here, tile_len)
        per_block = jnp.einsum(
            "nbk,mbk->bnm",
            scl_all.reshape(members, block_count, block_len),
            inc_all.reshape(members, block_count, block_len),
            precision=EXACT,
        )
        mixing = jnp.einsum("tb,bnm->tnm", mask_now, per_block, precision=EXACT)
        change = jnp.einsum("tnm,nti->mti", mixing, deviation, precision=EXACT).reshape(
            members, cell_count
        )
        ensemble = ensemble + change
    return ensemble


def solution(mesh):
    return jax.shard_map(
        local,
        mesh=mesh,
        in_specs=(
            P("mem", "cols"),
            P(None, "cols"),
            P(None, "cols"),
            P(None, "cols", None),
            P(None, "cols"),
            P(None, "cols", None),
            P(None, "cols"),
            P(("cols", "mem"), None, None),
        ),
        out_specs=P(None, ("cols", "mem")),
        check_vma=False,
    )
```

profile of v0, /device:TPU:1, one launch (start us, length us, event | category | flops | bytes accessed | tf_op | source)
XLA Modules:
  0.0 840.1 jit_solution(13650649832202001526)
XLA Ops:
  10.0 7.9 scatter_fusion.1
  19.1 12.0 %all-to-all-start.2 = ((f32[4,32,2,2]{0,3,2,1:T(2,128)}), f32[4,32,2,2]{0,3,2,1:T(2,128)S(1)}, u32[]{:S(2)}, u32[]{:S(2)}) async-start(f32[4,32,2,2]{0,3,2,1:T(2,128)} %copy.270), calls=%async_computation.2 | async-start | bytes 131072 | tf_op jit(solution)/shard_map/all_to_all | solution.py:66
  31.9 7.9 scatter_fusion
  40.5 1.2 copy.348
  41.8 2.2 copy.253
  44.0 9.2 %all-to-all-start.1 = ((s32[4,32,2,7]{3,2,0,1:T(2,128)}), s32[4,32,2,7]{3,2,0,1:T(2,128)S(1)}, u32[]{:S(2)}, u32[]{:S(2)}) async-start(s32[4,32,2,7]{3,2,0,1:T(2,128)} %copy.261), calls=%async_computation.1 | async-start | bytes 262144 | tf_op jit(solution)/shard_map/all_to_all | solution.py:63
  54.2 8.2 all-to-all-done.1
  62.4 7.1 all-to-all-start
  76.7 19.1 %all-to-all-done = f32[10,8,4096]{2,0,1:T(8,128)S(1)} async-done(((f32[10,8,4096]{2,0,1:T(8,128)}), f32[10,8,4096]{2,0,1:T(8,128)S(1)}, u32[]{:S(2)}, u32[]{:S(2)}) %all-to-all-start) | async-done | bytes 1310752 | tf_op jit(solution)/shard_map/all_to_all | solution.py:76
  95.9 1.8 copy.266
  97.8 2.4 gather_fusion
  101.2 21.2 %psum.84 = f32[80,64]{0,1:T(8,128)S(1)} all-reduce(f32[80,64]{0,1:T(8,128)S(1)} %broadcast_multiply_fusion.3), channel_id=1, replica_groups=mesh['cols'=32,'mem'=8] {'mem'}, use_global_device_ids=true, to_apply=%region_4.6 | all-reduce | flops 5120 | bytes 40960 | tf_op jit(solution)/shard_map/psum | solution.py:84
  123.4 1.2 scatter_custom_fusion.3
  132.6 1.3 broadcast_subtract_fusion
  133.9 134.3 %all-reduce.15.cloned.1.call-done = (f32[80,8,128]{2,0,1:T(8,128)}, f32[80,8,128]{2,0,1:T(8,128)}) async-done(((f32[80,8,128]{2,0,1:T(8,128)}, f32[80,8,128]{2,0,1:T(8,128)}), (f32[80,8,128]{2,0,1:T(8,128)}, f32[80,8,128]{2,0,1:T(8,128)})) %all-reduce.15.cloned.1.call-update) | async-done | bytes 655376 | tf_op jit(solution)/shard_map/psum | solution.py:93
  268.2 1.8 fusion.125
  270.6 2.1 fusion
  272.8 1.2 copy-done.4
  274.0 1.2 add.373
  275.2 2.8 copy.284
  278.0 2.4 gather_fusion.1
  281.5 25.4 %psum.87 = f32[80,64]{0,1:T(8,128)S(1)} all-reduce(f32[80,64]{0,1:T(8,128)S(1)} %broadcast_multiply_fusion.2), channel_id=1, replica_groups=mesh['cols'=32,'mem'=8] {'mem'}, use_global_device_ids=true, to_apply=%region_14.16 | all-reduce | flops 5120 | bytes 40960 | tf_op jit(solution)/shard_map/psum | solution.py:84
  307.8 1.8 scatter_custom_fusion.5
  309.7 2.0 copy.288
  311.6 1.8 scatter_custom_fusion.4
  313.4 2.0 copy.286
  317.6 1.8 copy.278
  319.4 2.7 reshape.653
  322.1 1.9 add_reduce_fusion
  324.0 134.3 %all-reduce.13.cloned.1.call-done = (f32[80,8,128]{2,0,1:T(8,128)}, f32[80,8,128]{2,0,1:T(8,128)}) async-done(((f32[80,8,128]{2,0,1:T(8,128)}, f32[80,8,128]{2,0,1:T(8,128)}), (f32[80,8,128]{2,0,1:T(8,128)}, f32[80,8,128]{2,0,1:T(8,128)})) %all-reduce.13.cloned.1.call-update) | async-done | bytes 655376 | tf_op jit(solution)/shard_map/psum | solution.py:93
  458.3 1.7 fusion.126
  460.5 3.9 fusion.122
  464.5 1.2 copy-done.5
  469.4 25.4 %psum.90 = f32[80,64]{0,1:T(8,128)S(1)} all-reduce(f32[80,64]{0,1:T(8,128)S(1)} %broadcast_multiply_fusion.1), channel_id=1, replica_groups=mesh['cols'=32,'mem'=8] {'mem'}, use_global_device_ids=true, to_apply=%region_23.25 | all-reduce | flops 5120 | bytes 40960 | tf_op jit(solution)/shard_map/psum | solution.py:84
  500.2 142.6 %all-reduce.11.cloned.1.call-done = (f32[80,8,128]{2,0,1:T(8,128)}, f32[80,8,128]{2,0,1:T(8,128)}) async-done(((f32[80,8,128]{2,0,1:T(8,128)}, f32[80,8,128]{2,0,1:T(8,128)}), (f32[80,8,128]{2,0,1:T(8,128)}, f32[80,8,128]{2,0,1:T(8,128)})) %all-reduce.11.cloned.1.call-update) | async-done | bytes 655376 | tf_op jit(solution)/shard_map/psum | solution.py:93
  642.8 1.7 fusion.127
  645.0 1.4 fusion.10
  646.6 1.2 copy-done.7
  647.8 1.2 add.398
  649.0 2.8 copy.308
  651.8 2.3 gather_fusion.3
  654.4 25.4 %psum.93 = f32[80,64]{0,1:T(8,128)S(1)} all-reduce(f32[80,64]{0,1:T(8,128)S(1)} %broadcast_multiply_fusion), channel_id=1, replica_groups=mesh['cols'=32,'mem'=8] {'mem'}, use_global_device_ids=true, to_apply=%region_32.34 | all-reduce | flops 5120 | bytes 40960 | tf_op jit(solution)/shard_map/psum | solution.py:84
  680.1 1.4 scatter_custom_fusion.9
  684.6 142.9 %all-reduce.9.cloned.1.call-done = (f32[80,8,128]{2,0,1:T(8,128)}, f32[80,8,128]{2,0,1:T(8,128)}) async-done(((f32[80,8,128]{2,0,1:T(8,128)}, f32[80,8,128]{2,0,1:T(8,128)}), (f32[80,8,128]{2,0,1:T(8,128)}, f32[80,8,128]{2,0,1:T(8,128)})) %all-reduce.9.cloned.1.call-update) | async-done | bytes 655376 | tf_op jit(solution)/shard_map/psum | solution.py:93
  827.4 1.7 fusion.128
  829.7 1.4 convolution_bitcast_fusion
  831.2 1.2 copy-done.8
  832.4 1.2 add.410
  (200 shorter events, 43.3 us)
Async XLA Ops:
  6.5 25.4 %copy-start.10 = (s32[4,32,2,7]{3,2,1,0:T(2,128)S(1)}, s32[4,32,2,7]{3,2,1,0:T(2,128)}, u32[]{:S(2)}) copy-start(s32[4,32,2,7]{3,2,1,0:T(2,128)} %constant.122.clone.1) | copy-start | bytes 21508
  6.5 24.6 %copy-start.18 = (s32[8,4,8]{2,1,0:T(4,128)S(1)}, s32[8,4,8]{2,1,0:T(4,128)}, u32[]{:S(2)}) copy-start(s32[8,4,8]{2,1,0:T(4,128)} %param.21) | copy-start | bytes 3076
  6.5 25.2 %copy-start.40 = (s32[4,32]{1,0:T(4,128)S(1)}, s32[4,32]{1,0:T(4,128)}, u32[]{:S(2)}) copy-start(s32[4,32]{1,0:T(4,128)} %param.20) | copy-start | bytes 1540
  6.5 25.2 %copy-start.21 = (s32[4,32,4]{1,2,0:T(4,128)S(1)}, s32[4,32,4]{1,2,0:T(4,128)}, u32[]{:S(2)}) copy-start(s32[4,32,4]{1,2,0:T(4,128)} %param.19) | copy-start | bytes 6148
  6.5 25.2 %copy-start.41 = (s32[4,32]{1,0:T(4,128)S(1)}, s32[4,32]{1,0:T(4,128)}, u32[]{:S(2)}) copy-start(s32[4,32]{1,0:T(4,128)} %param.18) | copy-start | bytes 1540
  18.0 22.6 %copy-start.11 = (f32[10,32768]{1,0:T(8,128)S(1)}, f32[10,32768]{1,0:T(8,128)}, u32[]{:S(2)}) copy-start(f32[10,32768]{1,0:T(8,128)} %param.14) | copy-start | bytes 3932164
  19.1 25.0 %all-to-all-start.2 = ((f32[4,32,2,2]{0,3,2,1:T(2,128)}), f32[4,32,2,2]{0,3,2,1:T(2,128)S(1)}, u32[]{:S(2)}, u32[]{:S(2)}) async-start(f32[4,32,2,2]{0,3,2,1:T(2,128)} %copy.270), calls=%async_computation.2 | async-start | bytes 131072 | tf_op jit(solution)/shard_map/all_to_all | solution.py:66
  44.0 18.4 %all-to-all-start.1 = ((s32[4,32,2,7]{3,2,0,1:T(2,128)}), s32[4,32,2,7]{3,2,0,1:T(2,128)S(1)}, u32[]{:S(2)}, u32[]{:S(2)}) async-start(s32[4,32,2,7]{3,2,0,1:T(2,128)} %copy.261), calls=%async_computation.1 | async-start | bytes 262144 | tf_op jit(solution)/shard_map/all_to_all | solution.py:63
  62.4 33.3 %all-to-all-start = ((f32[10,8,4096]{2,0,1:T(8,128)}), f32[10,8,4096]{2,0,1:T(8,128)S(1)}, u32[]{:S(2)}, u32[]{:S(2)}) async-start(f32[10,8,4096]{2,0,1:T(8,128)} %copy.253), calls=%async_computation | async-start | bytes 4194304 | tf_op jit(solution)/shard_map/all_to_all | solution.py:76
  69.5 198.7 %all-reduce.15.cloned.1.call-start = ((), (), s32[]{:S(2)}) async-start(), calls=%async_computation.6 | async-start | bytes 1310720 | tf_op jit(solution)/shard_map/psum | solution.py:93
  71.1 24.6 %copy-start.12 = (s32[1,64,4]{2,1,0:T(8,128)}, s32[1,64,4]{2,1,0:T(8,128)S(1)}, u32[]{:S(2)}) copy-start(s32[1,64,4]{2,1,0:T(8,128)S(1)} %get-tuple-element.71) | copy-start | bytes 3076
  71.1 24.6 %copy-start.14 = (s32[1,64,4]{2,1,0:T(8,128)}, s32[1,64,4]{2,1,0:T(8,128)S(1)}, u32[]{:S(2)}) copy-start(s32[1,64,4]{2,1,0:T(8,128)S(1)} %get-tuple-element.68) | copy-start | bytes 3076
  95.9 1.9 copy-start.3
  124.5 3.3 copy-start.19
  124.6 3.3 copy-start.20
  124.6 3.3 copy-start.22
  124.6 3.3 copy-start.23
  124.6 3.3 copy-start.35
  124.6 3.3 copy-start.36
  124.6 3.9 copy-start.15
  124.6 4.5 copy-start.13
  125.6 5.8 copy-start.38
  125.6 5.9 copy-start.24
  127.6 330.6 %all-reduce.13.cloned.1.call-start = ((), (), s32[]{:S(2)}) async-start(), calls=%async_computation.5 | async-start | bytes 1310720 | tf_op jit(solution)/shard_map/psum | solution.py:93
  132.4 1.5 copy-start.1
  268.2 2.3 copy-start.9
  272.7 1.3 copy-start.4
  278.0 29.8 %copy-start.31 = (f32[64]{0:T(128)S(1)}, f32[64]{0:T(128)}, u32[]{:S(2)}) copy-start(f32[64]{0:T(128)} %get-tuple-element.32) | copy-start | bytes 772
  309.6 6.0 copy-start.25
  309.6 6.0 copy-start.27
  309.6 6.0 copy-start.28
  309.6 6.0 copy-start.29
  309.6 6.6 copy-start.39
  315.4 327.4 %all-reduce.11.cloned.1.call-start = ((), (), s32[]{:S(2)}) async-start(), calls=%async_computation.4 | async-start | bytes 1310720 | tf_op jit(solution)/shard_map/psum | solution.py:93
  324.0 136.5 %copy-start.2 = (f32[80,8,512]{2,1,0:T(8,128)S(1)}, f32[80,8,512]{2,1,0:T(8,128)}, u32[]{:S(2)}) copy-start(f32[80,8,512]{2,1,0:T(8,128)} %copy-done.1) | copy-start | bytes 3932164
  464.4 1.3 copy-start.5
  496.9 3.1 copy-start.37
  496.9 3.2 copy-start.26
  499.0 145.5 %copy-start.17 = (s32[8,1,8]{2,1,0:T(1,128)S(1)}, s32[8,1,8]{2,1,0:T(1,128)}, u32[]{:S(2)}) copy-start(s32[8,1,8]{2,1,0:T(1,128)} %get-tuple-element.75) | copy-start | bytes 772
  499.9 145.1 %copy-start = (f32[80,8,512]{2,0,1:T(8,128)S(1)}, f32[80,8,512]{2,0,1:T(8,128)}, u32[]{:S(2)}) copy-start(f32[80,8,512]{2,0,1:T(8,128)} %get-tuple-element.63) | copy-start | bytes 3932164
  500.0 327.5 %all-reduce.9.cloned.1.call-start = ((), (), s32[]{:S(2)}) async-start(), calls=%async_computation.3 | async-start | bytes 1310720 | tf_op jit(solution)/shard_map/psum | solution.py:93
  646.4 1.3 copy-start.7
  649.0 5.1 copy-start.34
  651.8 28.3 %copy-start.32 = (f32[64]{0:T(128)S(1)}, f32[64]{0:T(128)}, u32[]{:S(2)}) copy-start(f32[64]{0:T(128)} %get-tuple-element.42) | copy-start | bytes 772
  651.8 28.3 %copy-start.33 = (f32[64]{0:T(128)S(1)}, f32[64]{0:T(128)}, u32[]{:S(2)}) copy-start(f32[64]{0:T(128)} %get-tuple-element.43) | copy-start | bytes 772
  651.8 28.3 %copy-start.30 = (f32[64]{0:T(128)S(1)}, f32[64]{0:T(128)}, u32[]{:S(2)}) copy-start(f32[64]{0:T(128)} %get-tuple-element.30) | copy-start | bytes 772
  683.6 145.6 %copy-start.16 = (s32[8,1,8]{2,1,0:T(1,128)S(1)}, s32[8,1,8]{2,1,0:T(1,128)}, u32[]{:S(2)}) copy-start(s32[8,1,8]{2,1,0:T(1,128)} %get-tuple-element.74) | copy-start | bytes 772
  831.1 1.3 copy-start.8
  (1 other events, 1.1 us)
Sparse Core Ops, SparseCore 0:
  127.8 140.4 all-reduce.14
  315.5 142.7 all-reduce.12
  500.1 142.6 all-reduce.10
  684.7 142.7 all-reduce.8
where the time goes:
time: 845 us; the launch traced here: 840 us
  waiting for transfers between devices  581 us (69%)
  blocking collectives  97.3 us (12%)
  local copies, waits for them, and re-layouts  67.1 us (8%)
  other arithmetic  33.7 us (4%)
  starting transfers between devices  28.8 us (3%)
  matrix products  17.7 us (2%)
  between operations  14 us (2%)
    psum x4, waiting for transfers between devices, local(): inc_all, scl_all = lax.psum((placed_inc, placed_scl), 'cols')  554 us
    psum x4, blocking collectives, local(): lax.psum(jnp.sum(jnp.where(inside[None], picked, 0.0), axis=2) / pick_cou...  97.3 us
    all_to_all x1, waiting for transfers between devices, local(): lax.all_to_all(state, 'mem', split_axis=1, concat_axis=0, tiled=True)  19.1 us
  transfers between devices with their start and end apart: 7, of which 6 were waited for; matrix products, arithmetic and copies ran while one was open for 4% of the time, Pallas kernels for 0%

commit v1 on v0

v1 whole, which is shorter than its diff:
```python
import jax
import jax.numpy as jnp
from jax import lax
from jax.experimental import pallas as pl
from jax.experimental.pallas import tpu as pltpu
from jax.sharding import PartitionSpec as P

epsilon = 1e-05
MESH = pl.DeviceIdType.MESH
F32 = jnp.float32
BF = jnp.bfloat16
I32 = jnp.int32

NB = 4
NC = 32
NK = 8
MLOC = 10
M = 80
NY = 4
NZ = 8
TILE = 512
NT = 8
CELLS = 4096
RA = 40
RB = 24


def vm():
    return pl.BlockSpec(memory_space=pltpu.VMEM)


def sm():
    return pl.BlockSpec(memory_space=pltpu.SMEM)


def hbm():
    return pl.BlockSpec(memory_space=pl.ANY)


def iota(shape, axis):
    return lax.broadcasted_iota(I32, shape, axis)


def greet(c, k):
    bar = pltpu.get_barrier_semaphore()
    for d in range(1, NC):
        pl.semaphore_signal(bar, inc=1, device_id=(lax.rem(c + d, NC), k), device_id_type=MESH)
    for d in range(1, NK):
        pl.semaphore_signal(bar, inc=1, device_id=(c, lax.rem(k + d, NK)), device_id_type=MESH)
    pl.semaphore_wait(bar, NC - 1 + NK - 1)


def send(src, dst, ssem, rsem, dev):
    cp = pltpu.make_async_remote_copy(
        src_ref=src, dst_ref=dst, send_sem=ssem, recv_sem=rsem, device_id=dev, device_id_type=MESH
    )
    cp.start()
    return cp


def slots_kernel(m_ref, mk_ref, r_ref, mko_ref, ss, rs, ks, kr):
    c = lax.axis_index("cols")
    k = lax.axis_index("mem")
    greet(c, k)
    cps = []
    for d in range(1, NC):
        p = lax.rem(c + d, NC)
        cps.append(send(m_ref.at[p], r_ref.at[c], ss.at[d], rs.at[d], (p, k)))
    for d in range(1, NK):
        cps.append(send(mk_ref, mko_ref.at[k], ks.at[d], kr.at[d], (c, lax.rem(k + d, NK))))
    r_ref[c] = m_ref[c]
    mko_ref[k] = mk_ref[...]
    for cp in cps:
        cp.wait()


def slots_call(m, mk):
    return pl.pallas_call(
        slots_kernel,
        out_shape=(
            jax.ShapeDtypeStruct((NC, 1, 128), I32),
            jax.ShapeDtypeStruct((NK, 8, 128), I32),
        ),
        in_specs=[vm(), vm()],
        out_specs=(vm(), vm()),
        scratch_shapes=[
            pltpu.SemaphoreType.DMA((NC,)),
            pltpu.SemaphoreType.DMA((NC,)),
            pltpu.SemaphoreType.DMA((NK,)),
            pltpu.SemaphoreType.DMA((NK,)),
        ],
        compiler_params=pltpu.CompilerParams(collective_id=0, has_side_effects=True),
        name="slots",
    )(m, mk)


def prior_kernel(r_ref, mk_ref, st_ref, out_ref, xs):
    k = lax.axis_index("mem")
    lane = iota((MLOC, 128), 1)
    lane1 = iota((1, 128), 1)
    xs[...] = jnp.zeros_like(xs)
    for q in range(8):

        def body(s, acc):
            a, e0, e1, e2 = acc
            v = jnp.zeros((MLOC, 128), F32)
            for p in range(4):
                cell = r_ref[s, q * 4 + p]
                base = pl.multiple_of((cell >> 7) * 128, 128)
                hit = lane == (cell & 127)
                v = v + jnp.where(hit, st_ref[:, pl.ds(base, 128)], 0.0)
            tile = r_ref[s, q * 4] >> 9
            col = jnp.sum(v, axis=1, keepdims=True) * 0.25
            here = lane1 == s
            a = jnp.where(lane == s, col, a)
            e0 = jnp.where(here, mk_ref[tile, 3 * k], e0)
            e1 = jnp.where(here, mk_ref[tile, 3 * k + 1], e1)
            e2 = jnp.where(here, mk_ref[tile, 3 * k + 2], e2)
            return a, e0, e1, e2

        z = jnp.zeros((1, 128), I32)
        a, e0, e1, e2 = lax.fori_loop(
            0, NC, body, (jnp.zeros((MLOC, 128), F32), z, z, z), unroll=4
        )
        xs[16 * q : 16 * q + 10, :] = a
        xs[16 * q + 10 : 16 * q + 11, :] = e0.astype(F32)
        xs[16 * q + 11 : 16 * q + 12, :] = e1.astype(F32)
        xs[16 * q + 12 : 16 * q + 13, :] = e2.astype(F32)
    xt = jnp.transpose(xs[...])
    out_ref[...] = xt[:NC].reshape(NC, 1, 128)


def prior_call(r, mk, state):
    return pl.pallas_call(
        prior_kernel,
        out_shape=jax.ShapeDtypeStruct((NC, 1, 128), F32),
        in_specs=[sm(), sm(), vm()],
        out_specs=vm(),
        scratch_shapes=[pltpu.VMEM((128, 128), F32)],
        name="prior",
    )(r, mk, state)


def gather_kernel(
    z_ref, meta_ref, st_ref, g_ref, s_ref, rz,
    ss, rs, xs, xr, a1s, a1r, b1s, b1r, a2s, a2r, b2s, b2r, ps, pr, ts, tr, own,
):
    c = lax.axis_index("cols")
    k = lax.axis_index("mem")
    y = c // NZ
    z = lax.rem(c, NZ)
    x = k // 2
    core = lax.rem(k, 2)
    greet(c, k)
    rows = []
    for d in range(1, NC):
        p = lax.rem(c + d, NC)
        rows.append(send(z_ref.at[p], rz.at[c], ss.at[d], rs.at[d], (p, k)))
    rz[c] = z_ref[c]
    for cp in rows:
        cp.wait()
    got = rz[...].reshape(NC, 128)
    owner = meta_ref[0:1, :]
    slot = meta_ref[1:2, :]
    hot = jnp.where(iota((NC, 128), 0).astype(F32) == owner, 1.0, 0.0)
    full = lax.dot_general(
        got, hot, (((0,), (0,)), ((), ())),
        precision=lax.Precision.HIGHEST, preferred_element_type=F32,
    )
    blk = jnp.zeros((16, 128), F32)
    for q in range(8):
        blk = blk + jnp.where(slot == float(q), full[16 * q : 16 * q + 16, :], 0.0)
    first = blk[0:8]
    second = blk[8:16]
    row8 = iota((8, 128), 0)
    second = jnp.where(row8 == 5, meta_ref[2:3, :], second)
    second = jnp.where(row8 == 6, meta_ref[3:4, :], second)
    second = jnp.where(row8 == 7, meta_ref[4:5, :], second)
    quad = lax.rem(k, 4)
    turned = second
    for j in range(1, 4):
        turned = jnp.where(quad == j, pltpu.roll(second, 2 * j, 0), turned)
    r0 = pl.multiple_of(16 * k, 16)
    g_ref[y, z, pl.ds(r0, 8), :] = first
    g_ref[y, z, pl.ds(pl.multiple_of(r0 + 8, 8), 8), :] = turned
    mine = g_ref.at[y, z, pl.ds(r0, 16), :]
    step = []
    for d in range(1, NK):
        step.append(send(mine, mine, xs.at[d], xr.at[d], (c, lax.rem(k + d, NK))))
    for cp in step:
        cp.wait()
    moves = []
    for d in range(1, NK):
        p = lax.rem(k + d, NK)
        moves.append(
            send(
                st_ref.at[:, pl.ds(pl.multiple_of(p * CELLS, CELLS), CELLS)],
                s_ref.at[k], ts.at[d], tr.at[d], (c, p),
            )
        )
    keep = pltpu.make_async_copy(
        st_ref.at[:, pl.ds(pl.multiple_of(k * CELLS, CELLS), CELLS)], s_ref.at[k], own
    )
    keep.start()
    ra = pl.multiple_of(64 * core, 8)
    rb = pl.multiple_of(64 * core + RA, 8)
    a1 = g_ref.at[y, z, pl.ds(ra, RA), :]
    b1 = g_ref.at[y, z, pl.ds(rb, RB), :]
    first_a = []
    first_b = []
    for d in range(1, NZ):
        first_a.append(send(a1, a1, a1s.at[d], a1r.at[d], (y * NZ + lax.rem(z + d, NZ), k)))
    for d in range(1, NY):
        first_b.append(send(b1, b1, b1s.at[d], b1r.at[d], (lax.rem(y + d, NY) * NZ + z, k)))
    for cp in first_b:
        cp.wait()
    b2 = g_ref.at[:, z, pl.ds(rb, RB), :]
    second_b = []
    for d in range(1, NZ):
        second_b.append(send(b2, b2, b2s.at[d], b2r.at[d], (y * NZ + lax.rem(z + d, NZ), k)))
    for cp in first_a:
        cp.wait()
    a2 = g_ref.at[y, :, pl.ds(ra, RA), :]
    second_a = []
    for d in range(1, NY):
        second_a.append(send(a2, a2, a2s.at[d], a2r.at[d], (lax.rem(y + d, NY) * NZ + z, k)))
    for cp in second_b:
        cp.wait()
    for cp in second_a:
        cp.wait()
    pair = []
    for d in range(1, NC):
        p = lax.rem(c + d, NC)
        half = g_ref.at[p // NZ, lax.rem(p, NZ), pl.ds(ra, 64), :]
        pair.append(send(half, half, ps.at[d], pr.at[d], (c, k + 1 - 2 * core)))
    for cp in pair:
        cp.wait()
    keep.wait()
    for cp in moves:
        cp.wait()


def gather_call(z, meta, state):
    dma = pltpu.SemaphoreType.DMA
    return pl.pallas_call(
        gather_kernel,
        out_shape=(
            jax.ShapeDtypeStruct((NY, NZ, 128, 128), F32),
            jax.ShapeDtypeStruct((NK, MLOC, CELLS), F32),
        ),
        in_specs=[vm(), vm(), hbm()],
        out_specs=(vm(), hbm()),
        scratch_shapes=[
            pltpu.VMEM((NC, 1, 128), F32),
            dma((NC,)), dma((NC,)), dma((NK,)), dma((NK,)),
            dma((NZ,)), dma((NZ,)), dma((NY,)), dma((NY,)),
            dma((NY,)), dma((NY,)), dma((NZ,)), dma((NZ,)),
            dma((NC,)), dma((NC,)), dma((NK,)), dma((NK,)), dma(()),
        ],
        compiler_params=pltpu.CompilerParams(collective_id=1, has_side_effects=True),
        name="spread_out",
    )(z, meta, state)


def split(v):
    hi = v.astype(BF)
    lo = (v - hi.astype(F32)).astype(BF)
    return hi, lo


def mm(a, b, dims):
    return lax.dot_general(a, b, (dims, ((), ())), preferred_element_type=F32)


NN = ((1,), (0,))
NT_ = ((1,), (1,))
TN = ((0,), (0,))
WIDE = NB * 1024 + NT * 128
CH = 512


def extra_row(k, x):
    return 16 * k + 8 + (2 * (k % 4) + 2 + x) % 8


def window_kernel(g_ref, s_ref, mk_ref, out_ref, zz, mask, val, pp, pt, dh, dl, sp, tp):
    lane_group = iota((128, 128), 1) // 32
    sub = iota((8, 128), 0) // 2

    def assemble(blk, _):
        parts = [g_ref[4 * blk + u] for u in range(4)]
        for b in range(NB):
            v = parts[3]
            for u in range(3):
                v = jnp.where(lane_group == (b + u) % 4, parts[u], v)
            lanes = pl.ds(pl.multiple_of(b * 1024 + blk * 128, 128), 128)
            for kk in range(NK):
                zz[8 * kk : 8 * kk + 8, lanes] = v[16 * kk : 16 * kk + 8]
            for h in range(2):
                t = v[16 * (4 * h) + 8 : 16 * (4 * h) + 16]
                for j in range(1, 4):
                    kk = 4 * h + j
                    t = jnp.where(sub == j, v[16 * kk + 8 : 16 * kk + 16], t)
                zz[64 + 8 * h : 72 + 8 * h, lanes] = t
            for e in range(8 * b):
                r = extra_row(e // 3, e % 3)
                mask[e : e + 1, lanes] = v[r : r + 1]
            for j in range(3):
                r = extra_row(0, 3 + j)
                val[j : j + 1, lanes] = v[r : r + 1]
        return 0

    lax.fori_loop(0, 8, assemble, 0)
    n = lax.rem(iota((M, NT * 128), 1), 128)
    kk = n // 16
    ii = lax.rem(n, 16)
    place = jnp.where(ii < 8, 8 * kk + ii, 64 + 2 * kk + ii - 8)
    unit = (iota((M, NT * 128), 0) == place) & (ii < MLOC)
    zz[:, NB * 1024 :] = jnp.where(unit, 1.0, 0.0)
    grow = jnp.where(iota((8, NT * 128), 0) == iota((8, NT * 128), 1) // 128, 1.0, 0.0)
    mask[:, NB * 1024 :] = mm(mk_ref[...].astype(F32), grow, TN)[:32]
    pp[...] = jnp.zeros_like(pp)

    for b in range(NB):
        lanes = slice(b * 1024, b * 1024 + 1024)
        prior = zz[:, lanes]
        accepted = val[0:1, lanes]
        observed = val[1:2, lanes]
        noise = val[2:3, lanes]
        mean = jnp.sum(prior, axis=0, keepdims=True) / M
        dev = prior - mean
        var = jnp.sum(dev * dev, axis=0, keepdims=True) / (M - 1) + epsilon
        den = var + noise
        shift = var / den * (observed - mean)
        factor = jnp.sqrt(noise / den) - 1.0
        inc = accepted * (shift + factor * dev)
        scl = dev / ((M - 1) * var)
        ih, il = split(inc)
        sh, sl = split(scl)
        for q in range(8):
            w = slice(128 * q, 128 * q + 128)
            prod = mm(sh[:, w], ih[:, w], NT_) + mm(sh[:, w], il[:, w], NT_) + mm(sl[:, w], ih[:, w], NT_)
            pp[80 * q : 80 * q + 80, 0:80] = prod
        ph, plo = split(jnp.transpose(pp[...])[:M])
        pt[0:M, :] = ph
        pt[M : 2 * M, :] = plo

        def update(i, _):
            at = pl.ds(pl.multiple_of((b + 1) * 1024 + i * CH, CH), CH)
            v = zz[:, at]
            d = v - jnp.sum(v, axis=0, keepdims=True) * (1.0 / M)
            hi, lo = split(d)
            for q in range(8):
                w = jnp.broadcast_to(mask[8 * b + q : 8 * b + q + 1, at], (16, CH)).astype(BF)
                for g in range(5):
                    rr = slice(80 * q + 16 * g, 80 * q + 16 * g + 16)
                    dh[rr, :] = hi[16 * g : 16 * g + 16] * w
                    dl[rr, :] = lo[16 * g : 16 * g + 16] * w
            both = mm(pt[...], dh[...], NN)
            rest = mm(pt[0:M, :], dl[...], NN)
            zz[:, at] = v + (both[0:M] + (both[M : 2 * M] + rest))
            return 0

        lax.fori_loop(0, (WIDE - (b + 1) * 1024) // CH, update, 0)

    true = iota((M, M), 0)
    tk = true // MLOC
    ti = lax.rem(true, MLOC)
    place = jnp.where(ti < 8, 8 * tk + ti, 64 + 2 * tk + ti - 8)
    perm = jnp.where(iota((M, M), 1) == place, 1.0, 0.0).astype(BF)
    th, tl = split(zz[:, NB * 1024 :])
    tp[0:M, :] = mm(perm, th, NN).astype(BF)
    tp[M : 2 * M, :] = mm(perm, tl, NN).astype(BF)
    sp[...] = jnp.zeros_like(sp)
    for t in range(NT):
        at = slice(TILE * t, TILE * t + TILE)
        for kk in range(NK):
            sp[16 * kk : 16 * kk + MLOC, :] = s_ref[kk, :, at]
        hi, lo = split(sp[...])
        maps = tp[:, 128 * t : 128 * t + 128]
        both = mm(maps, hi, NN)
        rest = mm(maps[0:M], lo, NN)
        out_ref[:, at] = both[0:M] + (both[M : 2 * M] + rest)


def window_call(g, s, mk):
    return pl.pallas_call(
        window_kernel,
        out_shape=jax.ShapeDtypeStruct((M, CELLS), F32),
        in_specs=[vm(), vm(), vm()],
        out_specs=vm(),
        scratch_shapes=[
            pltpu.VMEM((M, WIDE), F32),
            pltpu.VMEM((32, WIDE), F32),
            pltpu.VMEM((8, NB * 1024), F32),
            pltpu.VMEM((640, 128), F32),
            pltpu.VMEM((2 * M, 640), BF),
            pltpu.VMEM((640, CH), BF),
            pltpu.VMEM((640, CH), BF),
            pltpu.VMEM((128, TILE), F32),
            pltpu.VMEM((2 * M, NT * 128), BF),
        ],
        name="window",
    )(g, s, mk)


def prepare(obs_value, obs_var, owner, tile_of, offsets, accept, loc_mask, source):
    dest = owner[:, :, 0]
    order = jnp.arange(32, dtype=I32)
    same = (dest[:, :, None] == dest[:, None, :]) & (order[None, :] < order[:, None])[None]
    rank = jnp.sum(same.astype(I32), axis=2)
    cells = tile_of[:, :, None] * TILE + offsets
    hit = (dest[None, :, None, :] == order[:, None, None, None]) & (
        rank[None, :, None, :] == jnp.arange(2, dtype=I32)[None, None, :, None]
    )
    slots = jnp.sum(jnp.where(hit[:, :, :, :, None], cells[None, :, None, :, :], 0), axis=3)
    slots = jnp.pad(slots.reshape(NC, 32), ((0, 0), (0, 96))).reshape(NC, 1, 128)
    batch = jnp.arange(NB, dtype=I32)
    rows = jnp.stack(
        [
            dest.astype(F32),
            (batch[:, None] * 2 + rank).astype(F32),
            accept.astype(F32),
            obs_value,
            obs_var,
        ]
    )
    turn = jnp.mod(batch[:, None] - source, NB) == batch[None, :]
    meta = jnp.sum(jnp.where(turn[None, :, :, None], rows[:, None], 0.0), axis=2)
    meta = jnp.pad(meta.reshape(5, 128), ((0, 3), (0, 0)))
    mk = jnp.pad(loc_mask.reshape(8, 32), ((0, 0), (0, 96)))
    return slots, meta, mk


def local(state, obs_value, obs_var, owner, tile_of, offsets, accept, loc_mask):
    slots, meta, mk = prepare(
        obs_value, obs_var, owner, tile_of, offsets, accept, loc_mask, lax.axis_index("cols")
    )
    r, mks = slots_call(slots, mk)
    z = prior_call(r.reshape(NC, 128), mks.reshape(64, 128), state)
    g, s = gather_call(z, meta, state)
    return window_call(g.reshape(NC, 128, 128), s, mk)


def solution(mesh):
    return jax.shard_map(
        local,
        mesh=mesh,
        in_specs=(
            P("mem", "cols"),
            P(None, "cols"),
            P(None, "cols"),
            P(None, "cols", None),
            P(None, "cols"),
            P(None, "cols", None),
            P(None, "cols"),
            P(("cols", "mem"), None, None),
        ),
        out_specs=P(None, ("cols", "mem")),
        check_vma=False,
    )
```

time: 845 us -> 96.2 us (0.11)
  waiting for transfers between devices: 581 us -> 0 us
  blocking collectives: 97.3 us -> 0 us
  Pallas kernels: 0 us -> 86 us
  local copies, waits for them, and re-layouts: 67.1 us -> 4.15 us
  starting transfers between devices: 28.8 us -> 0 us
  other arithmetic: 33.7 us -> 5.37 us
  matrix products: 17.7 us -> 0 us
  between operations: 14 us -> 0.05 us
    psum x4 -> x0, waiting for transfers between devices: 554 us -> none  [local(): inc_all, scl_all = lax.psum((placed_inc, placed_scl), 'cols')]
    psum x4 -> x0, blocking collectives: 97.3 us -> none  [local(): lax.psum(jnp.sum(jnp.where(inside[None], picked, 0.0), axis=2) / pick_cou...]
    pallas_call x0 -> x4, Pallas kernels: none -> 86 us  [the longest x1 43.3 us: gather_call(): pl.pallas_call(gather_kernel, out_shape=(jax.ShapeDtypeStruct((NY, NZ, 12...]
    all_to_all x3 -> x0, starting transfers between devices: 28.3 us -> none  [the longest x1 12 us: local(): lax.all_to_all(sent_val, 'cols', split_axis=1, concat_axis=1, tiled=True)]
    all_to_all x3 -> x0, waiting for transfers between devices: 27.3 us -> none  [the longest x1 19.1 us: local(): lax.all_to_all(state, 'mem', split_axis=1, concat_axis=0, tiled=True)]
    dot_general x12 -> x0, matrix products: 17.7 us -> none  [the longest x4 8.78 us: local(): jnp.einsum('tnm,nti->mti', mixing, deviation, precision=EXACT)]
    scatter x4 -> x0, local copies, waits for them, and re-layouts: 17.6 us -> none  [the longest x2 9.02 us: local(): blank_val.at[batch_rows, destination, slot_rank]]
    reshape x13 -> x3, local copies, waits for them, and re-layouts: 12.6 us -> 0.95 us  [the longest x1 0.8 us: prepare(): mk = jnp.pad(loc_mask.reshape(8, 32), ((0, 0), (0, 96)))]
  transfers between devices with their start and end apart: 7 -> 0, of which waited for: 6 -> 0; matrix products, arithmetic and copies ran while one was open for 4% -> 0% of each run, Pallas kernels for 0% -> 0%
where the time goes in v1:
time: 96.2 us; the launch traced here: 95.5 us
  Pallas kernels  86 us (89%)
  other arithmetic  5.37 us (6%)
  local copies, waits for them, and re-layouts  4.15 us (4%)
    pallas_call x1, Pallas kernels, gather_call(): pl.pallas_call(gather_kernel, out_shape=(jax.ShapeDtypeStruct((NY, NZ, 12...  43.3 us
    pallas_call x1, Pallas kernels, slots_call(): pl.pallas_call(slots_kernel, out_shape=(jax.ShapeDtypeStruct((NC, 1, 128)...  17.8 us
    pallas_call x1, Pallas kernels, window_call(): pl.pallas_call(window_kernel, out_shape=jax.ShapeDtypeStruct((M, CELLS),...  15.5 us
    pallas_call x1, Pallas kernels, prior_call(): pl.pallas_call(prior_kernel, out_shape=jax.ShapeDtypeStruct((NC, 1, 128),...  9.36 us

profile of v1, /device:TPU:1, one launch (start us, length us, event | category | flops | bytes accessed | tf_op | source)
XLA Modules:
  0.0 95.5 jit_solution(17748475190382623140)
XLA Ops:
  0.0 0.1 iota_compare_fusion.3
  0.1 0.7 broadcast_multiply_fusion
  0.8 0.7 convert_element_type.32
  1.5 0.8 reshape.146
  2.3 0.6 pad.13.mk_ref
  2.9 1.0 %convert_reduce_fusion = s32[4,32]{1,0:T(4,128)S(1)} fusion(s32[4,32]{1,0:T(4,128)} %bitcast.23, pred[32,32]{1,0:T(8,128)(4,1)S(1)} %iota_compare_fusion.1), kind=kLoop, calls=%fused_computation.1 | loop fusion | flops 16256 | bytes 2048 | tf_op jit(solution)/shard_map/reduce_sum | solution.py:411
  3.9 0.7 broadcast_add_fusion
  4.6 0.1 constant_dynamic-update-slice_fusion.3
  4.6 0.7 constant_dynamic-update-slice_fusion.2
  5.3 0.7 constant_dynamic-update-slice_fusion.1
  6.0 0.7 constant_dynamic-update-slice_fusion
  6.7 0.1 select_reduce_fusion.1
  6.8 0.1 reshape.149
  6.9 0.6 pad.14.meta_ref
  7.5 0.7 iota_compare_fusion
  8.2 0.6 select_reduce_fusion
  8.9 0.1 copy.12
  8.9 0.6 pad.12
  9.6 17.8 %slots.1 = (s32[32,1,128]{2,1,0:T(1,128)}, s32[8,8,128]{2,1,0:T(8,128)}) custom-call(s32[32,1,128]{2,1,0:T(1,128)} %bitcast.21, s32[8,128]{1,0:T(8,128)} %pad.13.mk_ref), custom_call_target="tpu_custom_call" | custom-call | tf_op jit(solution)/shard_map/slots/pallas_call | solution.py:78
  27.3 9.4 %prior.1.z_ref = f32[32,1,128]{2,1,0:T(1,128)} custom-call(s32[32,128]{1,0:T(8,128)} %bitcast.25, s32[64,128]{1,0:T(8,128)} %bitcast.22, f32[10,32768]{1,0:T(8,128)} %st_ref.3), custom_call_target="tpu_custom_call" | custom-call | tf_op jit(solution)/shard_map/prior/pallas_call | solution.py:134
  36.7 43.3 %spread_out.1 = (f32[4,8,128,128]{3,2,1,0:T(8,128)}, f32[8,10,4096]{2,1,0:T(8,128)}) custom-call(f32[32,1,128]{2,1,0:T(1,128)} %prior.1.z_ref, f32[8,128]{1,0:T(8,128)} %pad.14.meta_ref, f32[10,32768]{1,0:T(8,128)} %st_ref.3), custom_call_target="tpu_custom_call" | custom-call | tf_op jit(solution)/shard_map/spread_out/pallas_call | solution.py:245
  80.0 15.5 %window.1 = f32[80,4096]{1,0:T(8,128)} custom-call(f32[32,128,128]{2,1,0:T(8,128)} %bitcast.19, f32[8,10,4096]{2,1,0:T(8,128)} %get-tuple-element.12.s_ref, s32[8,128]{1,0:T(8,128)} %pad.13.mk_ref), custom_call_target="tpu_custom_call" | custom-call | tf_op jit(solution)/shard_map/window/pallas_call | solution.py:387
  (6 shorter events, 0.1 us)

commit v2 on v1

v2 whole, which is shorter than its diff:
```python
import jax
import jax.numpy as jnp
from jax import lax
from jax.experimental import pallas as pl
from jax.experimental.pallas import tpu as pltpu
from jax.sharding import PartitionSpec as P

epsilon = 1e-05
MESH = pl.DeviceIdType.MESH
F32 = jnp.float32
BF = jnp.bfloat16
I32 = jnp.int32

NB = 4
NC = 32
NK = 8
MLOC = 10
M = 80
NY = 4
NZ = 8
TILE = 512
NT = 8
CELLS = 4096
RA = 40
RB = 24


def vm():
    return pl.BlockSpec(memory_space=pltpu.VMEM)


def sm():
    return pl.BlockSpec(memory_space=pltpu.SMEM)


def hbm():
    return pl.BlockSpec(memory_space=pl.ANY)


def iota(shape, axis):
    return lax.broadcasted_iota(I32, shape, axis)


def split(v):
    hi = v.astype(BF)
    lo = (v - hi.astype(F32)).astype(BF)
    return hi, lo


def mm(a, b, dims):
    return lax.dot_general(a, b, (dims, ((), ())), preferred_element_type=F32)


NN = ((1,), (0,))
NT_ = ((1,), (1,))
TN = ((0,), (0,))
def send(src, dst, ssem, rsem, dev):
    cp = pltpu.make_async_remote_copy(
        src_ref=src, dst_ref=dst, send_sem=ssem, recv_sem=rsem, device_id=dev, device_id_type=MESH
    )
    cp.start()
    return cp


def exchange_kernel(
    ow, ti, of, ac, va, vr, lm, st, g_ref, s_ref,
    stv, tiled, fi, fl, mv, mrow, rr, rsm, mks, xs, zrow, rz,
    ls, own, cs, ms, mr, ks, kr, ss, rs, xss, xsr, a1s, a1r, b1s, b1r, a2s, a2r, b2s, b2r,
    pas, par, pbs, pbr, pcs, pcr, pds, pdr, ts, tr,
):
    c = lax.axis_index("cols")
    k = lax.axis_index("mem")
    y = c // NZ
    z = lax.rem(c, NZ)
    core = lax.rem(k, 2)
    quad = lax.rem(k, 4)
    bar = pltpu.get_barrier_semaphore()
    for d in range(1, NC):
        pl.semaphore_signal(bar, inc=1, device_id=(lax.rem(c + d, NC), k), device_id_type=MESH)
    for d in range(1, NK):
        pl.semaphore_signal(bar, inc=1, device_id=(c, lax.rem(k + d, NK)), device_id_type=MESH)
    load = pltpu.make_async_copy(st, stv, ls)
    load.start()
    mv[...] = jnp.zeros_like(mv)
    tiles = ti[...] * TILE
    cells = [tiles + of[:, p, :] for p in range(4)]
    places = [ow[...], cells[0] + (cells[1] << 15), cells[2] + (cells[3] << 15)]
    fields = [ac[...].astype(F32), va[...], vr[...]]
    for b in range(NB):
        at = slice(32 * b, 32 * b + 32)
        for f in range(3):
            fi[f : f + 1, at] = places[f][b : b + 1, :]
            fl[f : f + 1, at] = fields[f][b : b + 1, :]
        mv[:, 8 * b : 8 * b + 8] = lm[:, b, :].astype(F32)
    r128 = iota((128, 128), 0)
    c128 = iota((128, 128), 1)
    lane32 = iota((NC, 128), 1)
    within = lane32 & 31
    hoti = jnp.where(iota((NC, 128), 0) == fi[0:1, :], 1, 0)
    seen = hoti
    for h in (1, 2, 4, 8, 16):
        seen = seen + jnp.where(within >= h, pltpu.roll(seen, h, 1), 0)
    slots = jnp.zeros((NC, 128), I32)
    for r in range(2):
        for w in range(2):
            v = jnp.where((hoti == 1) & (seen == r + 1), fi[w + 1 : w + 2, :], 0)
            for h in (1, 2, 4, 8, 16):
                v = v + pltpu.roll(v, 128 - h, 1)
            for p, cell in ((2 * w, v & 32767), (2 * w + 1, (v >> 15) & 32767)):
                for f, word in ((p, cell >> 7), (p + 4, cell & 127)):
                    spot = 8 * r + f
                    word = word if spot == 0 else pltpu.roll(word, spot, 1)
                    slots = jnp.where(within == spot, word, slots)
    mrow[...] = slots.reshape(NC, 1, 128)
    hot = hoti.astype(F32)
    rank = jnp.sum((hoti * (seen - 1)).astype(F32), axis=0, keepdims=True)
    load.wait()
    for t in range(NK * CELLS // 128):
        tiled[t] = stv[:, 128 * t : 128 * t + 128]
    pl.semaphore_wait(bar, NC - 1 + NK - 1)

    ask = []
    for d in range(1, NC):
        p = lax.rem(c + d, NC)
        ask.append(send(mrow.at[p], rr.at[c], ms.at[d], mr.at[d], (p, k)))
    maps = []
    for d in range(1, NK):
        maps.append(send(mv, mks.at[k], ks.at[d], kr.at[d], (c, lax.rem(k + d, NK))))
    rr[c] = mrow[c]
    mks[k] = mv[...]
    moves = []
    for d in range(1, NK):
        p = lax.rem(k + d, NK)
        part = stv.at[:, pl.ds(pl.multiple_of(p * CELLS, CELLS), CELLS)]
        moves.append(send(part, s_ref.at[k], ts.at[d], tr.at[d], (c, p)))
    keep = pltpu.make_async_copy(
        stv.at[:, pl.ds(pl.multiple_of(k * CELLS, CELLS), CELLS)], s_ref.at[k], own
    )
    keep.start()
    for cp in ask:
        cp.wait()
    scal = pltpu.make_async_copy(rr, rsm, cs)
    scal.start()
    for cp in maps:
        cp.wait()
    pick = lax.rem(c128, 16) - 10
    chosen = jnp.where((pick >= 0) & (pick < 3) & (r128 == 3 * k + pick), 1.0, 0.0)
    table = mm(mks[...].reshape(64, 128).astype(BF), chosen.astype(BF), NN).astype(BF)
    got = rr[...].reshape(NC, 128)
    extra = jnp.zeros((NC, 128), F32)
    for q in range(8):
        word = 32 * (q // 2) + 8 * (q % 2)
        tile = got[:, word : word + 1] >> 2
        at_tile = jnp.where(iota((NC, 64), 1) == tile, 1.0, 0.0).astype(BF)
        extra = jnp.where(lane32 // 16 == q, mm(at_tile, table, NN), extra)
    scal.wait()
    lane = iota((MLOC, 128), 1)

    def priors(i, accs):
        here = lane == i
        out = []
        for q in range(8):
            v = jnp.zeros((MLOC, 128), F32)
            word = 32 * (q // 2) + 8 * (q % 2)
            for p in range(4):
                hit = lane == rsm[i, 0, word + 4 + p]
                v = v + jnp.where(hit, tiled[rsm[i, 0, word + p]], 0.0)
            out.append(jnp.where(here, jnp.sum(v, axis=1, keepdims=True), accs[q]))
        return tuple(out)

    accs = lax.fori_loop(0, NC, priors, tuple(jnp.zeros((MLOC, 128), F32) for _ in range(8)))
    xs[...] = jnp.zeros_like(xs)
    for q in range(8):
        xs[16 * q : 16 * q + MLOC, :] = accs[q] * 0.25
    zr = jnp.transpose(xs[...])[:NC] + extra
    zrow[...] = zr.reshape(NC, 1, 128)
    back = []
    for d in range(1, NC):
        p = lax.rem(c + d, NC)
        back.append(send(zrow.at[p], rz.at[c], ss.at[d], rs.at[d], (p, k)))
    rz[c] = zrow[c]
    for cp in back:
        cp.wait()
    full = lax.dot_general(
        rz[...].reshape(NC, 128), hot, (TN, ((), ())),
        precision=lax.Precision.HIGHEST, preferred_element_type=F32,
    )
    batch = iota((1, 128), 1) // 32
    blk = jnp.zeros((16, 128), F32)
    for q in range(8):
        mine = (batch == q // 2) & (rank == float(q % 2))
        blk = blk + jnp.where(mine, full[16 * q : 16 * q + 16, :], 0.0)
    row16 = iota((16, 128), 0)
    for j in range(3):
        blk = jnp.where(row16 == 13 + j, fl[j : j + 1, :], blk)
    turned = blk
    around = lax.rem(z, 4)
    for j in range(1, 4):
        turned = jnp.where(around == j, pltpu.roll(blk, 32 * j, 1), turned)
    second = turned[8:16]
    placed = second
    for j in range(1, 4):
        placed = jnp.where(quad == j, pltpu.roll(second, 2 * j, 0), placed)
    r0 = pl.multiple_of(16 * k, 16)
    g_ref[y, z, pl.ds(r0, 8), :] = turned[0:8]
    g_ref[y, z, pl.ds(pl.multiple_of(r0 + 8, 8), 8), :] = placed
    block = g_ref.at[y, z, pl.ds(r0, 16), :]
    step = []
    for d in range(1, NK):
        step.append(send(block, block, xss.at[d], xsr.at[d], (c, lax.rem(k + d, NK))))
    for cp in step:
        cp.wait()
    ra = pl.multiple_of(64 * core, 8)
    rb = pl.multiple_of(64 * core + RA, 8)
    mate = (c, k + 1 - 2 * core)
    a1 = g_ref.at[y, z, pl.ds(ra, RA), :]
    b1 = g_ref.at[y, z, pl.ds(rb, RB), :]
    first_a = []
    first_b = []
    for d in range(1, NZ):
        first_a.append(send(a1, a1, a1s.at[d], a1r.at[d], (y * NZ + lax.rem(z + d, NZ), k)))
    for d in range(1, NY):
        first_b.append(send(b1, b1, b1s.at[d], b1r.at[d], (lax.rem(y + d, NY) * NZ + z, k)))
    for cp in first_b:
        cp.wait()
    b2 = g_ref.at[:, z, pl.ds(rb, RB), :]
    second_b = []
    for d in range(1, NZ):
        second_b.append(send(b2, b2, b2s.at[d], b2r.at[d], (y * NZ + lax.rem(z + d, NZ), k)))
    for cp in first_a:
        cp.wait()
    a2 = g_ref.at[y, :, pl.ds(ra, RA), :]
    second_a = []
    for d in range(1, NY):
        second_a.append(send(a2, a2, a2s.at[d], a2r.at[d], (lax.rem(y + d, NY) * NZ + z, k)))
    pair = []
    for d in range(1, NY):
        piece = g_ref.at[lax.rem(y + d, NY), z, pl.ds(rb, RB), :]
        pair.append(send(piece, piece, pas.at[d], par.at[d], mate))
    for d in range(1, NZ):
        piece = g_ref.at[y, lax.rem(z + d, NZ), pl.ds(ra, RA), :]
        pair.append(send(piece, piece, pbs.at[d], pbr.at[d], mate))
    for d in range(1, NZ):
        second_b[d - 1].wait_recv()
        piece = g_ref.at[:, lax.rem(z + NZ - d, NZ), pl.ds(rb, RB), :]
        pair.append(send(piece, piece, pcs.at[d], pcr.at[d], mate))
    for d in range(1, NY):
        second_a[d - 1].wait_recv()
        piece = g_ref.at[lax.rem(y + NY - d, NY), :, pl.ds(ra, RA), :]
        pair.append(send(piece, piece, pds.at[d], pdr.at[d], mate))
    for cp in second_b + second_a:
        cp.wait_send()
    keep.wait()
    for cp in moves + pair:
        cp.wait()


def exchange_call(ow, ti, of, ac, va, vr, lm, st):
    dma = pltpu.SemaphoreType.DMA
    row = pltpu.VMEM((NC, 1, 128), F32)
    irow = pltpu.VMEM((NC, 1, 128), I32)
    return pl.pallas_call(
        exchange_kernel,
        out_shape=(
            jax.ShapeDtypeStruct((NY, NZ, 128, 128), F32),
            jax.ShapeDtypeStruct((NK, MLOC, CELLS), F32),
        ),
        in_specs=[vm()] * 7 + [hbm()],
        out_specs=(vm(), hbm()),
        scratch_shapes=[
            pltpu.VMEM((MLOC, NK * CELLS), F32),
            pltpu.VMEM((NK * CELLS // 128, MLOC, 128), F32),
            pltpu.VMEM((8, 128), I32),
            pltpu.VMEM((8, 128), F32),
            pltpu.VMEM((8, 128), F32),
            irow, irow,
            pltpu.SMEM((NC, 1, 128), I32),
            pltpu.VMEM((NK, 8, 128), F32),
            pltpu.VMEM((128, 128), F32),
            row, row,
            dma(()), dma(()), dma(()),
            dma((NC,)), dma((NC,)), dma((NK,)), dma((NK,)),
            dma((NC,)), dma((NC,)), dma((NK,)), dma((NK,)),
            dma((NZ,)), dma((NZ,)), dma((NY,)), dma((NY,)),
            dma((NY,)), dma((NY,)), dma((NZ,)), dma((NZ,)),
            dma((NY,)), dma((NY,)), dma((NZ,)), dma((NZ,)),
            dma((NZ,)), dma((NZ,)), dma((NY,)), dma((NY,)),
            dma((NK,)), dma((NK,)),
        ],
        compiler_params=pltpu.CompilerParams(collective_id=0, has_side_effects=True),
        name="exchange",
    )(ow, ti, of, ac, va, vr, lm, st)


WIDE = NB * 1024 + NT * 128
CH = 512


def extra_row(k, x):
    return 16 * k + 8 + (2 * (k % 4) + 2 + x) % 8


def window_kernel(g_ref, s_ref, mk_ref, out_ref, zz, mask, val, pp, pt, dh, dl, sp, tp):
    lane_group = iota((128, 128), 1) // 32
    sub = iota((8, 128), 0) // 2

    def assemble(blk, _):
        parts = [g_ref[4 * blk + u] for u in range(4)]
        for b in range(NB):
            v = parts[3]
            for u in range(3):
                v = jnp.where(lane_group == (b + u) % 4, parts[u], v)
            lanes = pl.ds(pl.multiple_of(b * 1024 + blk * 128, 128), 128)
            for kk in range(NK):
                zz[8 * kk : 8 * kk + 8, lanes] = v[16 * kk : 16 * kk + 8]
            for h in range(2):
                t = v[16 * (4 * h) + 8 : 16 * (4 * h) + 16]
                for j in range(1, 4):
                    kk = 4 * h + j
                    t = jnp.where(sub == j, v[16 * kk + 8 : 16 * kk + 16], t)
                zz[64 + 8 * h : 72 + 8 * h, lanes] = t
            for e in range(8 * b):
                r = extra_row(e // 3, e % 3)
                mask[e : e + 1, lanes] = v[r : r + 1]
            for j in range(3):
                r = extra_row(0, 3 + j)
                val[j : j + 1, lanes] = v[r : r + 1]
        return 0

    lax.fori_loop(0, 8, assemble, 0)
    n = lax.rem(iota((M, NT * 128), 1), 128)
    kk = n // 16
    ii = lax.rem(n, 16)
    place = jnp.where(ii < 8, 8 * kk + ii, 64 + 2 * kk + ii - 8)
    unit = (iota((M, NT * 128), 0) == place) & (ii < MLOC)
    zz[:, NB * 1024 :] = jnp.where(unit, 1.0, 0.0)
    grow = jnp.where(iota((8, NT * 128), 0) == iota((8, NT * 128), 1) // 128, 1.0, 0.0)
    for b in range(NB):
        mask[8 * b : 8 * b + 8, NB * 1024 :] = mm(mk_ref[:, b, :].astype(F32), grow, TN)
    pp[...] = jnp.zeros_like(pp)

    for b in range(NB):
        lanes = slice(b * 1024, b * 1024 + 1024)
        prior = zz[:, lanes]
        accepted = val[0:1, lanes]
        observed = val[1:2, lanes]
        noise = val[2:3, lanes]
        mean = jnp.sum(prior, axis=0, keepdims=True) / M
        dev = prior - mean
        var = jnp.sum(dev * dev, axis=0, keepdims=True) / (M - 1) + epsilon
        den = var + noise
        shift = var / den * (observed - mean)
        factor = jnp.sqrt(noise / den) - 1.0
        inc = accepted * (shift + factor * dev)
        scl = dev / ((M - 1) * var)
        ih, il = split(inc)
        sh, sl = split(scl)
        for q in range(8):
            w = slice(128 * q, 128 * q + 128)
            prod = mm(sh[:, w], ih[:, w], NT_) + mm(sh[:, w], il[:, w], NT_) + mm(sl[:, w], ih[:, w], NT_)
            pp[80 * q : 80 * q + 80, 0:80] = prod
        ph, plo = split(jnp.transpose(pp[...])[:M])
        pt[0:M, :] = ph
        pt[M : 2 * M, :] = plo

        def update(i, _):
            at = pl.ds(pl.multiple_of((b + 1) * 1024 + i * CH, CH), CH)
            v = zz[:, at]
            d = v - jnp.sum(v, axis=0, keepdims=True) * (1.0 / M)
            hi, lo = split(d)
            for q in range(8):
                w = jnp.broadcast_to(mask[8 * b + q : 8 * b + q + 1, at], (16, CH)).astype(BF)
                for g in range(5):
                    rr = slice(80 * q + 16 * g, 80 * q + 16 * g + 16)
                    dh[rr, :] = hi[16 * g : 16 * g + 16] * w
                    dl[rr, :] = lo[16 * g : 16 * g + 16] * w
            both = mm(pt[...], dh[...], NN)
            rest = mm(pt[0:M, :], dl[...], NN)
            zz[:, at] = v + (both[0:M] + (both[M : 2 * M] + rest))
            return 0

        lax.fori_loop(0, (WIDE - (b + 1) * 1024) // CH, update, 0)

    true = iota((M, M), 0)
    tk = true // MLOC
    ti = lax.rem(true, MLOC)
    place = jnp.where(ti < 8, 8 * tk + ti, 64 + 2 * tk + ti - 8)
    perm = jnp.where(iota((M, M), 1) == place, 1.0, 0.0).astype(BF)
    th, tl = split(zz[:, NB * 1024 :])
    tp[0:M, :] = mm(perm, th, NN).astype(BF)
    tp[M : 2 * M, :] = mm(perm, tl, NN).astype(BF)
    sp[...] = jnp.zeros_like(sp)
    for t in range(NT):
        at = slice(TILE * t, TILE * t + TILE)
        for kk in range(NK):
            sp[16 * kk : 16 * kk + MLOC, :] = s_ref[kk, :, at]
        hi, lo = split(sp[...])
        maps = tp[:, 128 * t : 128 * t + 128]
        both = mm(maps, hi, NN)
        rest = mm(maps[0:M], lo, NN)
        out_ref[:, at] = both[0:M] + (both[M : 2 * M] + rest)


def window_call(g, s, mk):
    return pl.pallas_call(
        window_kernel,
        out_shape=jax.ShapeDtypeStruct((M, CELLS), F32),
        in_specs=[vm(), vm(), vm()],
        out_specs=vm(),
        scratch_shapes=[
            pltpu.VMEM((M, WIDE), F32),
            pltpu.VMEM((32, WIDE), F32),
            pltpu.VMEM((8, NB * 1024), F32),
            pltpu.VMEM((640, 128), F32),
            pltpu.VMEM((2 * M, 640), BF),
            pltpu.VMEM((640, CH), BF),
            pltpu.VMEM((640, CH), BF),
            pltpu.VMEM((128, TILE), F32),
            pltpu.VMEM((2 * M, NT * 128), BF),
        ],
        name="window",
    )(g, s, mk)


def local(state, obs_value, obs_var, owner, tile_of, offsets, accept, loc_mask):
    places = jnp.transpose(offsets, (0, 2, 1))
    g, s = exchange_call(
        owner[:, :, 0], tile_of, places, accept, obs_value, obs_var, loc_mask, state
    )
    return window_call(g.reshape(NC, 128, 128), s, loc_mask)


def solution(mesh):
    return jax.shard_map(
        local,
        mesh=mesh,
        in_specs=(
            P("mem", "cols"),
            P(None, "cols"),
            P(None, "cols"),
            P(None, "cols", None),
            P(None, "cols"),
            P(None, "cols", None),
            P(None, "cols"),
            P(("cols", "mem"), None, None),
        ),
        out_specs=P(None, ("cols", "mem")),
        check_vma=False,
    )
```

time: 96.2 us -> 76.4 us (0.79)
  Pallas kernels: 86 us -> 76.2 us
  other arithmetic: 5.37 us -> 0 us
  local copies, waits for them, and re-layouts: 4.15 us -> 0 us
    pallas_call x3 -> x1, Pallas kernels: 70.5 us -> 60.7 us  [exchange_call(): pl.pallas_call(exchange_kernel, out_shape=(jax.ShapeDtypeStruct((NY, NZ,...]
    pad x3 -> x0, local copies, waits for them, and re-layouts: 1.82 us -> none  [the longest x1 0.62 us: prepare(): jnp.pad(slots.reshape(NC, 32), ((0, 0), (0, 96))).reshape(NC, 1, 128)]
    reduce_sum x3 -> x0, other arithmetic: 1.71 us -> none  [the longest x1 0.97 us: prepare(): rank = jnp.sum(same.astype(I32), axis=2)]
where the time goes in v2:
time: 76.4 us; the launch traced here: 76.2 us
  Pallas kernels  76.2 us (100%)
    pallas_call x1, Pallas kernels, exchange_call(): pl.pallas_call(exchange_kernel, out_shape=(jax.ShapeDtypeStruct((NY, NZ,...  60.7 us
    pallas_call x1, Pallas kernels, window_call(): pl.pallas_call(window_kernel, out_shape=jax.ShapeDtypeStruct((M, CELLS),...  15.5 us

profile of v2, /device:TPU:1, one launch (start us, length us, event | category | flops | bytes accessed | tf_op | source)
XLA Modules:
  0.0 76.2 jit_solution(1084704141325443493)
XLA Ops:
  0.0 60.7 %exchange.1 = (f32[4,8,128,128]{3,2,1,0:T(8,128)}, f32[8,10,4096]{2,1,0:T(8,128)}) custom-call(s32[4,32]{1,0:T(4,128)} %bitcast.5, s32[4,32]{1,0:T(4,128)} %ti.1, s32[4,4,32]{2,1,0:T(4,128)} %bitcast.4, s32[4,32]{1,0:T(4,128)} %ac.1, f32[4,32]{1,0:T(4,128)} %va.1, f32[4,32]{1,0:T(4,128)} %vr.1, s32[8,4,8]{2,1,0:T(4,128)} %mk_ref.1, f32[10,32768]{1,0:T(8,128)} %st.1), custom_call_target="tpu_custom_call" | custom-call | tf_op jit(solution)/shard_map/exchange/pallas_call | solution.py:262
  60.7 15.5 %window.1 = f32[80,4096]{1,0:T(8,128)} custom-call(f32[32,128,128]{2,1,0:T(8,128)} %bitcast.3, f32[8,10,4096]{2,1,0:T(8,128)} %get-tuple-element.8.s_ref, s32[8,4,8]{2,1,0:T(4,128)} %mk_ref.1), custom_call_target="tpu_custom_call" | custom-call | tf_op jit(solution)/shard_map/window/pallas_call | solution.py:405

commit v3 on v2

--- a/solution.py
+++ b/solution.py
@@ -60,6 +60,15 @@
     )
     cp.start()
     return cp
+
+
+FAR = sorted(
+    ((dy, dz) for dy in range(NY) for dz in range(NZ) if dy + dz > 0),
+    key=lambda o: -(min(o[0], NY - o[0]) + min(o[1], NZ - o[1])),
+)
+FAR_K = (4, 3, 5, 2, 6, 1, 7)
+EARLY = (4, 2, 7, 1)
+LATE = (5, 3, 6)
 
 
 def exchange_kernel(
@@ -75,9 +84,10 @@
     core = lax.rem(k, 2)
     quad = lax.rem(k, 4)
     bar = pltpu.get_barrier_semaphore()
-    for d in range(1, NC):
-        pl.semaphore_signal(bar, inc=1, device_id=(lax.rem(c + d, NC), k), device_id_type=MESH)
-    for d in range(1, NK):
+    cols = [(dy * NZ + dz, lax.rem(y + dy, NY) * NZ + lax.rem(z + dz, NZ)) for dy, dz in FAR]
+    for d, p in cols:
+        pl.semaphore_signal(bar, inc=1, device_id=(p, k), device_id_type=MESH)
+    for d in FAR_K:
         pl.semaphore_signal(bar, inc=1, device_id=(c, lax.rem(k + d, NK)), device_id_type=MESH)
     load = pltpu.make_async_copy(st, stv, ls)
     load.start()
@@ -120,32 +130,32 @@
     pl.semaphore_wait(bar, NC - 1 + NK - 1)
 
     ask = []
-    for d in range(1, NC):
-        p = lax.rem(c + d, NC)
+    for d, p in cols:
         ask.append(send(mrow.at[p], rr.at[c], ms.at[d], mr.at[d], (p, k)))
     maps = []
-    for d in range(1, NK):
+    for d in FAR_K:
         maps.append(send(mv, mks.at[k], ks.at[d], kr.at[d], (c, lax.rem(k + d, NK))))
     rr[c] = mrow[c]
     mks[k] = mv[...]
-    moves = []
-    for d in range(1, NK):
+    def move(d):
         p = lax.rem(k + d, NK)
         part = stv.at[:, pl.ds(pl.multiple_of(p * CELLS, CELLS), CELLS)]
-        moves.append(send(part, s_ref.at[k], ts.at[d], tr.at[d], (c, p)))
+        return send(part, s_ref.at[k], ts.at[d], tr.at[d], (c, p))
+
+    moves = [move(d) for d in EARLY]
     keep = pltpu.make_async_copy(
         stv.at[:, pl.ds(pl.multiple_of(k * CELLS, CELLS), CELLS)], s_ref.at[k], own
     )
     keep.start()
-    for cp in ask:
-        cp.wait()
-    scal = pltpu.make_async_copy(rr, rsm, cs)
-    scal.start()
     for cp in maps:
         cp.wait()
     pick = lax.rem(c128, 16) - 10
     chosen = jnp.where((pick >= 0) & (pick < 3) & (r128 == 3 * k + pick), 1.0, 0.0)
     table = mm(mks[...].reshape(64, 128).astype(BF), chosen.astype(BF), NN).astype(BF)
+    for cp in ask:
+        cp.wait()
+    scal = pltpu.make_async_copy(rr, rsm, cs)
+    scal.start()
     got = rr[...].reshape(NC, 128)
     extra = jnp.zeros((NC, 128), F32)
     for q in range(8):
@@ -168,15 +178,14 @@
             out.append(jnp.where(here, jnp.sum(v, axis=1, keepdims=True), accs[q]))
         return tuple(out)
 
-    accs = lax.fori_loop(0, NC, priors, tuple(jnp.zeros((MLOC, 128), F32) for _ in range(8)))
+    accs = lax.fori_loop(0, NC, priors, tuple(jnp.zeros((MLOC, 128), F32) for _ in range(8)), unroll=4)
     xs[...] = jnp.zeros_like(xs)
     for q in range(8):
         xs[16 * q : 16 * q + MLOC, :] = accs[q] * 0.25
     zr = jnp.transpose(xs[...])[:NC] + extra
     zrow[...] = zr.reshape(NC, 1, 128)
     back = []
-    for d in range(1, NC):
-        p = lax.rem(c + d, NC)
+    for d, p in cols:
         back.append(send(zrow.at[p], rz.at[c], ss.at[d], rs.at[d], (p, k)))
     rz[c] = zrow[c]
     for cp in back:
@@ -206,10 +215,11 @@
     g_ref[y, z, pl.ds(pl.multiple_of(r0 + 8, 8), 8), :] = placed
     block = g_ref.at[y, z, pl.ds(r0, 16), :]
     step = []
-    for d in range(1, NK):
+    for d in FAR_K:
         step.append(send(block, block, xss.at[d], xsr.at[d], (c, lax.rem(k + d, NK))))
     for cp in step:
         cp.wait()
+    moves += [move(d) for d in LATE]
     ra = pl.multiple_of(64 * core, 8)
     rb = pl.multiple_of(64 * core + RA, 8)
     mate = (c, k + 1 - 2 * core)
@@ -300,11 +310,18 @@
     return 16 * k + 8 + (2 * (k % 4) + 2 + x) % 8
 
 
-def window_kernel(g_ref, s_ref, mk_ref, out_ref, zz, mask, val, pp, pt, dh, dl, sp, tp):
+def window_kernel(g_hbm, s_hbm, mk_ref, out, zz, mask, val, pp, pt, dh, dl, sp, tp, g_ref, s_ref, out_ref, gsem, ssem, osem):
+    gets = [pltpu.make_async_copy(g_hbm.at[pl.ds(4 * q, 4)], g_ref.at[pl.ds(4 * q, 4)], gsem.at[q]) for q in range(8)]
+    for cp in gets:
+        cp.start()
+    state = pltpu.make_async_copy(s_hbm, s_ref, ssem)
+    state.start()
     lane_group = iota((128, 128), 1) // 32
     sub = iota((8, 128), 0) // 2
 
     def assemble(blk, _):
+        part = pl.ds(4 * blk, 4)
+        pltpu.make_async_copy(g_hbm.at[part], g_ref.at[part], gsem.at[blk]).wait()
         parts = [g_ref[4 * blk + u] for u in range(4)]
         for b in range(NB):
             v = parts[3]
@@ -390,6 +407,8 @@
     tp[0:M, :] = mm(perm, th, NN).astype(BF)
     tp[M : 2 * M, :] = mm(perm, tl, NN).astype(BF)
     sp[...] = jnp.zeros_like(sp)
+    state.wait()
+    puts = []
     for t in range(NT):
         at = slice(TILE * t, TILE * t + TILE)
         for kk in range(NK):
@@ -399,14 +418,18 @@
         both = mm(maps, hi, NN)
         rest = mm(maps[0:M], lo, NN)
         out_ref[:, at] = both[0:M] + (both[M : 2 * M] + rest)
+        puts.append(pltpu.make_async_copy(out_ref.at[:, at], out.at[:, at], osem.at[t]))
+        puts[-1].start()
+    for cp in puts:
+        cp.wait()
 
 
 def window_call(g, s, mk):
     return pl.pallas_call(
         window_kernel,
         out_shape=jax.ShapeDtypeStruct((M, CELLS), F32),
-        in_specs=[vm(), vm(), vm()],
-        out_specs=vm(),
+        in_specs=[hbm(), hbm(), vm()],
+        out_specs=hbm(),
         scratch_shapes=[
             pltpu.VMEM((M, WIDE), F32),
             pltpu.VMEM((32, WIDE), F32),
@@ -417,6 +440,12 @@
             pltpu.VMEM((640, CH), BF),
             pltpu.VMEM((128, TILE), F32),
             pltpu.VMEM((2 * M, NT * 128), BF),
+            pltpu.VMEM((NC, 128, 128), F32),
+            pltpu.VMEM((NK, MLOC, CELLS), F32),
+            pltpu.VMEM((M, CELLS), F32),
+            pltpu.SemaphoreType.DMA((8,)),
+            pltpu.SemaphoreType.DMA(()),
+            pltpu.SemaphoreType.DMA((NT,)),
         ],
         name="window",
     )(g, s, mk)

time: 76.4 us -> 68.3 us (0.89)
  Pallas kernels: 76.2 us -> 68 us
    pallas_call x1, Pallas kernels: 60.7 us -> 53.1 us  [exchange_call(): pl.pallas_call(exchange_kernel, out_shape=(jax.ShapeDtypeStruct((NY, NZ,...]
where the time goes in v3:
time: 68.3 us; the launch traced here: 68 us
  Pallas kernels  68 us (100%)
    pallas_call x1, Pallas kernels, exchange_call(): pl.pallas_call(exchange_kernel, out_shape=(jax.ShapeDtypeStruct((NY, NZ,...  53.1 us
    pallas_call x1, Pallas kernels, window_call(): pl.pallas_call(window_kernel, out_shape=jax.ShapeDtypeStruct((M, CELLS),...  14.9 us

profile of v3, /device:TPU:1, one launch (start us, length us, event | category | flops | bytes accessed | tf_op | source)
XLA Modules:
  0.0 68.0 jit_solution(5329794598906217712)
XLA Ops:
  0.0 53.1 %exchange.1 = (f32[4,8,128,128]{3,2,1,0:T(8,128)}, f32[8,10,4096]{2,1,0:T(8,128)}) custom-call(s32[4,32]{1,0:T(4,128)} %bitcast.5, s32[4,32]{1,0:T(4,128)} %ti.1, s32[4,4,32]{2,1,0:T(4,128)} %bitcast.4, s32[4,32]{1,0:T(4,128)} %ac.1, f32[4,32]{1,0:T(4,128)} %va.1, f32[4,32]{1,0:T(4,128)} %vr.1, s32[8,4,8]{2,1,0:T(4,128)} %mk_ref.1, f32[10,32768]{1,0:T(8,128)} %st.1), custom_call_target="tpu_custom_call" | custom-call | tf_op jit(solution)/shard_map/exchange/pallas_call | solution.py:272
  53.1 14.9 %window.1 = f32[80,4096]{1,0:T(8,128)} custom-call(f32[32,128,128]{2,1,0:T(8,128)} %bitcast.3, f32[8,10,4096]{2,1,0:T(8,128)} %get-tuple-element.8.s_hbm, s32[8,4,8]{2,1,0:T(4,128)} %mk_ref.1), custom_call_target="tpu_custom_call" | custom-call | tf_op jit(solution)/shard_map/window/pallas_call | solution.py:428

commit v4 on v3

--- a/solution.py
+++ b/solution.py
@@ -67,6 +67,8 @@
     key=lambda o: -(min(o[0], NY - o[0]) + min(o[1], NZ - o[1])),
 )
 FAR_K = (4, 3, 5, 2, 6, 1, 7)
+NEAR_Y = (1, 3, 2)
+NEAR_Z = (1, 7, 2, 6, 3, 5, 4)
 EARLY = (4, 2, 7, 1)
 LATE = (5, 3, 6)
 
@@ -75,7 +77,7 @@
     ow, ti, of, ac, va, vr, lm, st, g_ref, s_ref,
     stv, tiled, fi, fl, mv, mrow, rr, rsm, mks, xs, zrow, rz,
     ls, own, cs, ms, mr, ks, kr, ss, rs, xss, xsr, a1s, a1r, b1s, b1r, a2s, a2r, b2s, b2r,
-    pas, par, pbs, pbr, pcs, pcr, pds, pdr, ts, tr,
+    pas, par, ts, tr,
 ):
     c = lax.axis_index("cols")
     k = lax.axis_index("mem")
@@ -178,7 +180,7 @@
             out.append(jnp.where(here, jnp.sum(v, axis=1, keepdims=True), accs[q]))
         return tuple(out)
 
-    accs = lax.fori_loop(0, NC, priors, tuple(jnp.zeros((MLOC, 128), F32) for _ in range(8)), unroll=4)
+    accs = lax.fori_loop(0, NC, priors, tuple(jnp.zeros((MLOC, 128), F32) for _ in range(8)), unroll=True)
     xs[...] = jnp.zeros_like(xs)
     for q in range(8):
         xs[16 * q : 16 * q + MLOC, :] = accs[q] * 0.25
@@ -219,47 +221,67 @@
         step.append(send(block, block, xss.at[d], xsr.at[d], (c, lax.rem(k + d, NK))))
     for cp in step:
         cp.wait()
-    moves += [move(d) for d in LATE]
     ra = pl.multiple_of(64 * core, 8)
     rb = pl.multiple_of(64 * core + RA, 8)
     mate = (c, k + 1 - 2 * core)
-    a1 = g_ref.at[y, z, pl.ds(ra, RA), :]
-    b1 = g_ref.at[y, z, pl.ds(rb, RB), :]
-    first_a = []
-    first_b = []
-    for d in range(1, NZ):
-        first_a.append(send(a1, a1, a1s.at[d], a1r.at[d], (y * NZ + lax.rem(z + d, NZ), k)))
-    for d in range(1, NY):
-        first_b.append(send(b1, b1, b1s.at[d], b1r.at[d], (lax.rem(y + d, NY) * NZ + z, k)))
-    for cp in first_b:
-        cp.wait()
-    b2 = g_ref.at[:, z, pl.ds(rb, RB), :]
-    second_b = []
-    for d in range(1, NZ):
-        second_b.append(send(b2, b2, b2s.at[d], b2r.at[d], (y * NZ + lax.rem(z + d, NZ), k)))
-    for cp in first_a:
-        cp.wait()
-    a2 = g_ref.at[y, :, pl.ds(ra, RA), :]
-    second_a = []
-    for d in range(1, NY):
-        second_a.append(send(a2, a2, a2s.at[d], a2r.at[d], (lax.rem(y + d, NY) * NZ + z, k)))
+    y_at = [lax.rem(y + d, NY) for d in range(NY)]
+    z_at = [lax.rem(z + d, NZ) for d in range(NZ)]
+
+    def piece_a(dy, dz):
+        return g_ref.at[y_at[(-dy) % NY], z_at[(-dz) % NZ], pl.ds(ra, RA), :]
+
+    def piece_b(dy, dz):
+        return g_ref.at[y_at[(-dy) % NY], z_at[(-dz) % NZ], pl.ds(rb, RB), :]
+
+    out_a = {}
+    out_b = {}
     pair = []
-    for d in range(1, NY):
-        piece = g_ref.at[lax.rem(y + d, NY), z, pl.ds(rb, RB), :]
-        pair.append(send(piece, piece, pas.at[d], par.at[d], mate))
-    for d in range(1, NZ):
-        piece = g_ref.at[y, lax.rem(z + d, NZ), pl.ds(ra, RA), :]
-        pair.append(send(piece, piece, pbs.at[d], pbr.at[d], mate))
-    for d in range(1, NZ):
-        second_b[d - 1].wait_recv()
-        piece = g_ref.at[:, lax.rem(z + NZ - d, NZ), pl.ds(rb, RB), :]
-        pair.append(send(piece, piece, pcs.at[d], pcr.at[d], mate))
-    for d in range(1, NY):
-        second_a[d - 1].wait_recv()
-        piece = g_ref.at[lax.rem(y + NY - d, NY), :, pl.ds(ra, RA), :]
-        pair.append(send(piece, piece, pds.at[d], pdr.at[d], mate))
-    for cp in second_b + second_a:
-        cp.wait_send()
+
+    def along_y(e):
+        piece = piece_a(0, e)
+        for d in NEAR_Y:
+            out_a[d, e] = send(piece, piece, a2s.at[d, e], a2r.at[d, e], (y_at[d] * NZ + z, k))
+
+    def along_z(e):
+        piece = piece_b(e, 0)
+        for d in NEAR_Z:
+            out_b[d, e] = send(piece, piece, b2s.at[d, e], b2r.at[d, e], (y * NZ + z_at[d], k))
+
+    def to_mate(piece, n, dy, dz):
+        pair.append(send(piece, piece, pas.at[n, dy, dz], par.at[n, dy, dz], mate))
+
+    own_a = piece_a(0, 0)
+    own_b = piece_b(0, 0)
+    first_a = {}
+    first_b = {}
+    for d in NEAR_Z:
+        first_a[d] = send(own_a, own_a, a1s.at[d], a1r.at[d], (y * NZ + z_at[d], k))
+    for d in NEAR_Y:
+        first_b[d] = send(own_b, own_b, b1s.at[d], b1r.at[d], (y_at[d] * NZ + z, k))
+    along_y(0)
+    along_z(0)
+    moves += [move(d) for d in LATE]
+    for kind, e in (("b", 1), ("a", 1), ("b", 3), ("a", 7), ("a", 2), ("b", 2), ("a", 6), ("a", 3), ("a", 5), ("a", 4)):
+        if kind == "a":
+            first_a[e].wait_recv()
+            along_y(e)
+            to_mate(piece_a(0, e), 0, 0, e)
+        else:
+            first_b[e].wait_recv()
+            along_z(e)
+            to_mate(piece_b(e, 0), 1, e, 0)
+    order = [(0, d, e) for d in NEAR_Y for e in range(NZ)] + [(1, e, d) for d in NEAR_Z for e in range(NY)]
+    order.sort(key=lambda o: (min(o[1], NY - o[1]) + min(o[2], NZ - o[2])))
+    for n, dy, dz in order:
+        if n == 0:
+            out_a[dy, dz].wait_recv()
+            to_mate(piece_a(dy, dz), 0, dy, dz)
+        else:
+            out_b[dz, dy].wait_recv()
+            to_mate(piece_b(dy, dz), 1, dy, dz)
+    for group in (first_a, first_b, out_a, out_b):
+        for cp in group.values():
+            cp.wait_send()
     keep.wait()
     for cp in moves + pair:
         cp.wait()
@@ -292,9 +314,8 @@
             dma((NC,)), dma((NC,)), dma((NK,)), dma((NK,)),
             dma((NC,)), dma((NC,)), dma((NK,)), dma((NK,)),
             dma((NZ,)), dma((NZ,)), dma((NY,)), dma((NY,)),
-            dma((NY,)), dma((NY,)), dma((NZ,)), dma((NZ,)),
-            dma((NY,)), dma((NY,)), dma((NZ,)), dma((NZ,)),
-            dma((NZ,)), dma((NZ,)), dma((NY,)), dma((NY,)),
+            dma((NY, NZ)), dma((NY, NZ)), dma((NZ, NY)), dma((NZ, NY)),
+            dma((2, NY, NZ)), dma((2, NY, NZ)),
             dma((NK,)), dma((NK,)),
         ],
         compiler_params=pltpu.CompilerParams(collective_id=0, has_side_effects=True),

time: 68.3 us -> 67.4 us (0.987)
  Pallas kernels: 68 us -> 67.1 us
    pallas_call x1, Pallas kernels: 53.1 us -> 52.2 us  [exchange_call(): pl.pallas_call(exchange_kernel, out_shape=(jax.ShapeDtypeStruct((NY, NZ,...]
where the time goes in v4:
time: 67.4 us; the launch traced here: 67.1 us
  Pallas kernels  67.1 us (100%)
    pallas_call x1, Pallas kernels, exchange_call(): pl.pallas_call(exchange_kernel, out_shape=(jax.ShapeDtypeStruct((NY, NZ,...  52.2 us
    pallas_call x1, Pallas kernels, window_call(): pl.pallas_call(window_kernel, out_shape=jax.ShapeDtypeStruct((M, CELLS),...  14.9 us

profile of v4, /device:TPU:1, one launch (start us, length us, event | category | flops | bytes accessed | tf_op | source)
XLA Modules:
  0.0 67.1 jit_solution(16790811343271517413)
XLA Ops:
  0.0 52.2 %exchange.1 = (f32[4,8,128,128]{3,2,1,0:T(8,128)}, f32[8,10,4096]{2,1,0:T(8,128)}) custom-call(s32[4,32]{1,0:T(4,128)} %bitcast.5, s32[4,32]{1,0:T(4,128)} %ti.1, s32[4,4,32]{2,1,0:T(4,128)} %bitcast.4, s32[4,32]{1,0:T(4,128)} %ac.1, f32[4,32]{1,0:T(4,128)} %va.1, f32[4,32]{1,0:T(4,128)} %vr.1, s32[8,4,8]{2,1,0:T(4,128)} %mk_ref.1, f32[10,32768]{1,0:T(8,128)} %st.1), custom_call_target="tpu_custom_call" | custom-call | tf_op jit(solution)/shard_map/exchange/pallas_call | solution.py:294
  52.2 14.9 %window.1 = f32[80,4096]{1,0:T(8,128)} custom-call(f32[32,128,128]{2,1,0:T(8,128)} %bitcast.3, f32[8,10,4096]{2,1,0:T(8,128)} %get-tuple-element.8.s_hbm, s32[8,4,8]{2,1,0:T(4,128)} %mk_ref.1), custom_call_target="tpu_custom_call" | custom-call | tf_op jit(solution)/shard_map/window/pallas_call | solution.py:449

commit v5 on v4

--- a/solution.py
+++ b/solution.py
@@ -21,8 +21,8 @@
 TILE = 512
 NT = 8
 CELLS = 4096
-RA = 40
-RB = 24
+RA = 48
+RB = 16
 
 
 def vm():
@@ -323,7 +323,8 @@
     )(ow, ti, of, ac, va, vr, lm, st)
 
 
-WIDE = NB * 1024 + NT * 128
+MAPS = NT * M
+WIDE = NB * 1024 + MAPS
 CH = 512
 
 
@@ -331,7 +332,7 @@
     return 16 * k + 8 + (2 * (k % 4) + 2 + x) % 8
 
 
-def window_kernel(g_hbm, s_hbm, mk_ref, out, zz, mask, val, pp, pt, dh, dl, sp, tp, g_ref, s_ref, out_ref, gsem, ssem, osem):
+def window_kernel(g_hbm, s_hbm, mk_ref, out, zz, mask, val, pp, pt, dh, dl, th, tl, sp, tp, g_ref, s_ref, out_ref, gsem, ssem, osem):
     gets = [pltpu.make_async_copy(g_hbm.at[pl.ds(4 * q, 4)], g_ref.at[pl.ds(4 * q, 4)], gsem.at[q]) for q in range(8)]
     for cp in gets:
         cp.start()
@@ -366,13 +367,9 @@
         return 0
 
     lax.fori_loop(0, 8, assemble, 0)
-    n = lax.rem(iota((M, NT * 128), 1), 128)
-    kk = n // 16
-    ii = lax.rem(n, 16)
-    place = jnp.where(ii < 8, 8 * kk + ii, 64 + 2 * kk + ii - 8)
-    unit = (iota((M, NT * 128), 0) == place) & (ii < MLOC)
+    unit = lax.rem(iota((M, MAPS), 1), M) == iota((M, MAPS), 0)
     zz[:, NB * 1024 :] = jnp.where(unit, 1.0, 0.0)
-    grow = jnp.where(iota((8, NT * 128), 0) == iota((8, NT * 128), 1) // 128, 1.0, 0.0)
+    grow = jnp.where(iota((8, MAPS), 0) == iota((8, MAPS), 1) // M, 1.0, 0.0)
     for b in range(NB):
         mask[8 * b : 8 * b + 8, NB * 1024 :] = mm(mk_ref[:, b, :].astype(F32), grow, TN)
     pp[...] = jnp.zeros_like(pp)
@@ -389,53 +386,58 @@
         den = var + noise
         shift = var / den * (observed - mean)
         factor = jnp.sqrt(noise / den) - 1.0
-        inc = accepted * (shift + factor * dev)
-        scl = dev / ((M - 1) * var)
+        inc = accepted * shift + (accepted * factor) * dev
+        scl = dev * (1.0 / ((M - 1) * var))
         ih, il = split(inc)
         sh, sl = split(scl)
         for q in range(8):
             w = slice(128 * q, 128 * q + 128)
-            prod = mm(sh[:, w], ih[:, w], NT_) + mm(sh[:, w], il[:, w], NT_) + mm(sl[:, w], ih[:, w], NT_)
-            pp[80 * q : 80 * q + 80, 0:80] = prod
-        ph, plo = split(jnp.transpose(pp[...])[:M])
-        pt[0:M, :] = ph
-        pt[M : 2 * M, :] = plo
-
-        def update(i, _):
-            at = pl.ds(pl.multiple_of((b + 1) * 1024 + i * CH, CH), CH)
+            left = jnp.concatenate([sh[:, w], sl[:, w]], axis=1)
+            right = jnp.concatenate([ih[:, w], ih[:, w]], axis=1)
+            prod = mm(left, right, NT_) + mm(sh[:, w], il[:, w], NT_)
+            pp[b % 2, 80 * q : 80 * q + 80, 0:80] = prod
+        ph, plo = split(jnp.transpose(pp[b % 2])[:M])
+        pt[b, 0:M, :] = ph
+        pt[b, M : 2 * M, :] = plo
+
+        def change(at, wide, dh, dl, b=b):
             v = zz[:, at]
             d = v - jnp.sum(v, axis=0, keepdims=True) * (1.0 / M)
             hi, lo = split(d)
             for q in range(8):
-                w = jnp.broadcast_to(mask[8 * b + q : 8 * b + q + 1, at], (16, CH)).astype(BF)
+                w = jnp.broadcast_to(mask[8 * b + q : 8 * b + q + 1, at], (16, wide)).astype(BF)
                 for g in range(5):
                     rr = slice(80 * q + 16 * g, 80 * q + 16 * g + 16)
                     dh[rr, :] = hi[16 * g : 16 * g + 16] * w
                     dl[rr, :] = lo[16 * g : 16 * g + 16] * w
-            both = mm(pt[...], dh[...], NN)
-            rest = mm(pt[0:M, :], dl[...], NN)
+            both = mm(pt[b], dh[...], NN)
+            rest = mm(pt[b, 0:M, :], dl[...], NN)
             zz[:, at] = v + (both[0:M] + (both[M : 2 * M] + rest))
+
+        def update(i, _):
+            change(pl.ds(pl.multiple_of((b + 1) * 1024 + i * CH, CH), CH), CH, dh, dl)
             return 0
 
-        lax.fori_loop(0, (WIDE - (b + 1) * 1024) // CH, update, 0)
+        lax.fori_loop(0, (NB - 1 - b) * 1024 // CH, update, 0)
+        change(slice(NB * 1024, WIDE), MAPS, th, tl)
 
     true = iota((M, M), 0)
     tk = true // MLOC
     ti = lax.rem(true, MLOC)
     place = jnp.where(ti < 8, 8 * tk + ti, 64 + 2 * tk + ti - 8)
     perm = jnp.where(iota((M, M), 1) == place, 1.0, 0.0).astype(BF)
-    th, tl = split(zz[:, NB * 1024 :])
-    tp[0:M, :] = mm(perm, th, NN).astype(BF)
-    tp[M : 2 * M, :] = mm(perm, tl, NN).astype(BF)
-    sp[...] = jnp.zeros_like(sp)
+    whole, part = split(zz[:, NB * 1024 :])
+    tp[0:M, :] = mm(perm, whole, NN).astype(BF)
+    tp[M : 2 * M, :] = mm(perm, part, NN).astype(BF)
     state.wait()
     puts = []
     for t in range(NT):
         at = slice(TILE * t, TILE * t + TILE)
         for kk in range(NK):
-            sp[16 * kk : 16 * kk + MLOC, :] = s_ref[kk, :, at]
-        hi, lo = split(sp[...])
-        maps = tp[:, 128 * t : 128 * t + 128]
+            sp[t % 2, 8 * kk : 8 * kk + 8, :] = s_ref[kk, 0:8, at]
+            sp[t % 2, 64 + 2 * kk : 66 + 2 * kk, :] = s_ref[kk, 8:10, at]
+        hi, lo = split(sp[t % 2])
+        maps = tp[:, M * t : M * t + M]
         both = mm(maps, hi, NN)
         rest = mm(maps[0:M], lo, NN)
         out_ref[:, at] = both[0:M] + (both[M : 2 * M] + rest)
@@ -455,12 +457,14 @@
             pltpu.VMEM((M, WIDE), F32),
             pltpu.VMEM((32, WIDE), F32),
             pltpu.VMEM((8, NB * 1024), F32),
-            pltpu.VMEM((640, 128), F32),
-            pltpu.VMEM((2 * M, 640), BF),
+            pltpu.VMEM((2, 640, 128), F32),
+            pltpu.VMEM((NB, 2 * M, 640), BF),
             pltpu.VMEM((640, CH), BF),
             pltpu.VMEM((640, CH), BF),
-            pltpu.VMEM((128, TILE), F32),
-            pltpu.VMEM((2 * M, NT * 128), BF),
+            pltpu.VMEM((640, MAPS), BF),
+            pltpu.VMEM((640, MAPS), BF),
+            pltpu.VMEM((2, M, TILE), F32),
+            pltpu.VMEM((2 * M, MAPS), BF),
             pltpu.VMEM((NC, 128, 128), F32),
             pltpu.VMEM((NK, MLOC, CELLS), F32),
             pltpu.VMEM((M, CELLS), F32),

time: 67.4 us -> 64.9 us (0.963)
  Pallas kernels: 67.1 us -> 64.6 us
    pallas_call x1, Pallas kernels: 14.9 us -> 12.4 us  [window_call(): pl.pallas_call(window_kernel, out_shape=jax.ShapeDtypeStruct((M, CELLS),...]
where the time goes in v5:
time: 64.9 us; the launch traced here: 64.6 us
  Pallas kernels  64.6 us (100%)
    pallas_call x1, Pallas kernels, exchange_call(): pl.pallas_call(exchange_kernel, out_shape=(jax.ShapeDtypeStruct((NY, NZ,...  52.2 us
    pallas_call x1, Pallas kernels, window_call(): pl.pallas_call(window_kernel, out_shape=jax.ShapeDtypeStruct((M, CELLS),...  12.4 us

profile of v5, /device:TPU:1, one launch (start us, length us, event | category | flops | bytes accessed | tf_op | source)
XLA Modules:
  0.0 64.6 jit_solution(6362040214726344349)
XLA Ops:
  0.0 52.2 %exchange.1 = (f32[4,8,128,128]{3,2,1,0:T(8,128)}, f32[8,10,4096]{2,1,0:T(8,128)}) custom-call(s32[4,32]{1,0:T(4,128)} %bitcast.5, s32[4,32]{1,0:T(4,128)} %ti.1, s32[4,4,32]{2,1,0:T(4,128)} %bitcast.4, s32[4,32]{1,0:T(4,128)} %ac.1, f32[4,32]{1,0:T(4,128)} %va.1, f32[4,32]{1,0:T(4,128)} %vr.1, s32[8,4,8]{2,1,0:T(4,128)} %mk_ref.1, f32[10,32768]{1,0:T(8,128)} %st.1), custom_call_target="tpu_custom_call" | custom-call | tf_op jit(solution)/shard_map/exchange/pallas_call | solution.py:294
  52.2 12.4 %window.1 = f32[80,4096]{1,0:T(8,128)} custom-call(f32[32,128,128]{2,1,0:T(8,128)} %bitcast.3, f32[8,10,4096]{2,1,0:T(8,128)} %get-tuple-element.8.s_hbm, s32[8,4,8]{2,1,0:T(4,128)} %mk_ref.1), custom_call_target="tpu_custom_call" | custom-call | tf_op jit(solution)/shard_map/window/pallas_call | solution.py:451

commit v6 on v5

--- a/solution.py
+++ b/solution.py
@@ -21,8 +21,10 @@
 TILE = 512
 NT = 8
 CELLS = 4096
-RA = 48
+RA = 40
 RB = 16
+HALF = RA + RB
+ROWS = 2 * HALF
 
 
 def vm():
@@ -74,17 +76,16 @@
 
 
 def exchange_kernel(
-    ow, ti, of, ac, va, vr, lm, st, g_ref, s_ref,
-    stv, tiled, fi, fl, mv, mrow, rr, rsm, mks, xs, zrow, rz,
+    ow, ti, of, ac, va, vr, lm, st, g_ref, s_ref, s2_ref,
+    stv, tiled, fi, fl, mv, mrow, rr, rsm, mks, xs, zrow, rz, blocks, tail,
     ls, own, cs, ms, mr, ks, kr, ss, rs, xss, xsr, a1s, a1r, b1s, b1r, a2s, a2r, b2s, b2r,
-    pas, par, ts, tr,
+    pas, par, ts, tr, us, ur, own2,
 ):
     c = lax.axis_index("cols")
     k = lax.axis_index("mem")
     y = c // NZ
     z = lax.rem(c, NZ)
     core = lax.rem(k, 2)
-    quad = lax.rem(k, 4)
     bar = pltpu.get_barrier_semaphore()
     cols = [(dy * NZ + dz, lax.rem(y + dy, NY) * NZ + lax.rem(z + dz, NZ)) for dy, dz in FAR]
     for d, p in cols:
@@ -129,6 +130,10 @@
     load.wait()
     for t in range(NK * CELLS // 128):
         tiled[t] = stv[:, 128 * t : 128 * t + 128]
+    for p in range(NK):
+        for j in range(4):
+            at = CELLS * p + 1024 * j
+            tail[p, 2 * j : 2 * j + 2, :] = stv[8:10, at : at + 1024]
     pl.semaphore_wait(bar, NC - 1 + NK - 1)
 
     ask = []
@@ -141,14 +146,19 @@
     mks[k] = mv[...]
     def move(d):
         p = lax.rem(k + d, NK)
-        part = stv.at[:, pl.ds(pl.multiple_of(p * CELLS, CELLS), CELLS)]
-        return send(part, s_ref.at[k], ts.at[d], tr.at[d], (c, p))
-
-    moves = [move(d) for d in EARLY]
+        part = stv.at[0:8, pl.ds(pl.multiple_of(p * CELLS, CELLS), CELLS)]
+        return [
+            send(part, s_ref.at[k], ts.at[d], tr.at[d], (c, p)),
+            send(tail.at[p], s2_ref.at[k], us.at[d], ur.at[d], (c, p)),
+        ]
+
+    moves = [cp for d in EARLY for cp in move(d)]
     keep = pltpu.make_async_copy(
-        stv.at[:, pl.ds(pl.multiple_of(k * CELLS, CELLS), CELLS)], s_ref.at[k], own
+        stv.at[0:8, pl.ds(pl.multiple_of(k * CELLS, CELLS), CELLS)], s_ref.at[k], own
     )
     keep.start()
+    keep2 = pltpu.make_async_copy(tail.at[k], s2_ref.at[k], own2)
+    keep2.start()
     for cp in maps:
         cp.wait()
     pick = lax.rem(c128, 16) - 10
@@ -208,21 +218,30 @@
     around = lax.rem(z, 4)
     for j in range(1, 4):
         turned = jnp.where(around == j, pltpu.roll(blk, 32 * j, 1), turned)
-    second = turned[8:16]
-    placed = second
-    for j in range(1, 4):
-        placed = jnp.where(quad == j, pltpu.roll(second, 2 * j, 0), placed)
-    r0 = pl.multiple_of(16 * k, 16)
-    g_ref[y, z, pl.ds(r0, 8), :] = turned[0:8]
-    g_ref[y, z, pl.ds(pl.multiple_of(r0 + 8, 8), 8), :] = placed
-    block = g_ref.at[y, z, pl.ds(r0, 16), :]
+    blocks[k] = turned
+    block = blocks.at[k]
     step = []
     for d in FAR_K:
         step.append(send(block, block, xss.at[d], xsr.at[d], (c, lax.rem(k + d, NK))))
     for cp in step:
         cp.wait()
-    ra = pl.multiple_of(64 * core, 8)
-    rb = pl.multiple_of(64 * core + RA, 8)
+    sub8 = iota((8, 128), 0)
+    for h in range(2):
+        tails = [blocks[4 * h + u, 8:16, :] for u in range(4)]
+        for u in range(4):
+            g_ref[y, z, HALF * h + 8 * u : HALF * h + 8 * u + 8, :] = blocks[4 * h + u, 0:8, :]
+        last = tails[0]
+        for u in range(1, 4):
+            last = jnp.where(sub8 // 2 == u, pltpu.roll(tails[u], 2 * u, 0), last)
+        g_ref[y, z, HALF * h + 32 : HALF * h + 40, :] = last
+        low = jnp.where(sub8 < 3, pltpu.roll(tails[0], 6, 0), pltpu.roll(tails[1], 1, 0))
+        low = jnp.where(sub8 >= 6, pltpu.roll(tails[0], 1, 0), low)
+        high = jnp.where(sub8 < 3, pltpu.roll(tails[2], 6, 0), pltpu.roll(tails[3], 1, 0))
+        high = jnp.where(sub8 >= 6, pltpu.roll(tails[2], 7, 0), high)
+        g_ref[y, z, HALF * h + 40 : HALF * h + 48, :] = low
+        g_ref[y, z, HALF * h + 48 : HALF * h + 56, :] = high
+    ra = pl.multiple_of(HALF * core, 8)
+    rb = pl.multiple_of(HALF * core + RA, 8)
     mate = (c, k + 1 - 2 * core)
     y_at = [lax.rem(y + d, NY) for d in range(NY)]
     z_at = [lax.rem(z + d, NZ) for d in range(NZ)]
@@ -260,7 +279,7 @@
         first_b[d] = send(own_b, own_b, b1s.at[d], b1r.at[d], (y_at[d] * NZ + z, k))
     along_y(0)
     along_z(0)
-    moves += [move(d) for d in LATE]
+    moves += [cp for d in LATE for cp in move(d)]
     for kind, e in (("b", 1), ("a", 1), ("b", 3), ("a", 7), ("a", 2), ("b", 2), ("a", 6), ("a", 3), ("a", 5), ("a", 4)):
         if kind == "a":
             first_a[e].wait_recv()
@@ -283,6 +302,7 @@
         for cp in group.values():
             cp.wait_send()
     keep.wait()
+    keep2.wait()
     for cp in moves + pair:
         cp.wait()
 
@@ -294,11 +314,12 @@
     return pl.pallas_call(
         exchange_kernel,
         out_shape=(
-            jax.ShapeDtypeStruct((NY, NZ, 128, 128), F32),
-            jax.ShapeDtypeStruct((NK, MLOC, CELLS), F32),
+            jax.ShapeDtypeStruct((NY, NZ, ROWS, 128), F32),
+            jax.ShapeDtypeStruct((NK, 8, CELLS), F32),
+            jax.ShapeDtypeStruct((NK, 8, 1024), F32),
         ),
         in_specs=[vm()] * 7 + [hbm()],
-        out_specs=(vm(), hbm()),
+        out_specs=(vm(), hbm(), hbm()),
         scratch_shapes=[
             pltpu.VMEM((MLOC, NK * CELLS), F32),
             pltpu.VMEM((NK * CELLS // 128, MLOC, 128), F32),
@@ -310,13 +331,15 @@
             pltpu.VMEM((NK, 8, 128), F32),
             pltpu.VMEM((128, 128), F32),
             row, row,
+            pltpu.VMEM((NK, 16, 128), F32),
+            pltpu.VMEM((NK, 8, 1024), F32),
             dma(()), dma(()), dma(()),
             dma((NC,)), dma((NC,)), dma((NK,)), dma((NK,)),
             dma((NC,)), dma((NC,)), dma((NK,)), dma((NK,)),
             dma((NZ,)), dma((NZ,)), dma((NY,)), dma((NY,)),
             dma((NY, NZ)), dma((NY, NZ)), dma((NZ, NY)), dma((NZ, NY)),
             dma((2, NY, NZ)), dma((2, NY, NZ)),
-            dma((NK,)), dma((NK,)),
+            dma((NK,)), dma((NK,)), dma((NK,)), dma((NK,)), dma(()),
         ],
         compiler_params=pltpu.CompilerParams(collective_id=0, has_side_effects=True),
         name="exchange",
@@ -328,18 +351,23 @@
 CH = 512
 
 
-def extra_row(k, x):
-    return 16 * k + 8 + (2 * (k % 4) + 2 + x) % 8
-
-
-def window_kernel(g_hbm, s_hbm, mk_ref, out, zz, mask, val, pp, pt, dh, dl, th, tl, sp, tp, g_ref, s_ref, out_ref, gsem, ssem, osem):
+def mask_row(e):
+    k, x = divmod(e, 3)
+    return HALF * (k // 4) + 40 + 8 * (k % 4 // 2) + 3 * (k % 2) + x
+
+
+VALUE_ROWS = (46, 47, 54)
+
+
+def window_kernel(g_hbm, s_hbm, s2_hbm, mk_ref, out, zz, mask, val, pp, pt, dh, dl, th, tl, sp, tp, g_ref, s_ref, s2_ref, out_ref, gsem, ssem, ssem2, osem):
     gets = [pltpu.make_async_copy(g_hbm.at[pl.ds(4 * q, 4)], g_ref.at[pl.ds(4 * q, 4)], gsem.at[q]) for q in range(8)]
     for cp in gets:
         cp.start()
     state = pltpu.make_async_copy(s_hbm, s_ref, ssem)
     state.start()
-    lane_group = iota((128, 128), 1) // 32
-    sub = iota((8, 128), 0) // 2
+    ends = pltpu.make_async_copy(s2_hbm, s2_ref, ssem2)
+    ends.start()
+    lane_group = iota((ROWS, 128), 1) // 32
 
     def assemble(blk, _):
         part = pl.ds(4 * blk, 4)
@@ -350,19 +378,13 @@
             for u in range(3):
                 v = jnp.where(lane_group == (b + u) % 4, parts[u], v)
             lanes = pl.ds(pl.multiple_of(b * 1024 + blk * 128, 128), 128)
-            for kk in range(NK):
-                zz[8 * kk : 8 * kk + 8, lanes] = v[16 * kk : 16 * kk + 8]
             for h in range(2):
-                t = v[16 * (4 * h) + 8 : 16 * (4 * h) + 16]
-                for j in range(1, 4):
-                    kk = 4 * h + j
-                    t = jnp.where(sub == j, v[16 * kk + 8 : 16 * kk + 16], t)
-                zz[64 + 8 * h : 72 + 8 * h, lanes] = t
+                zz[32 * h : 32 * h + 32, lanes] = v[HALF * h : HALF * h + 32]
+                zz[64 + 8 * h : 72 + 8 * h, lanes] = v[HALF * h + 32 : HALF * h + 40]
             for e in range(8 * b):
-                r = extra_row(e // 3, e % 3)
+                r = mask_row(e)
                 mask[e : e + 1, lanes] = v[r : r + 1]
-            for j in range(3):
-                r = extra_row(0, 3 + j)
+            for j, r in enumerate(VALUE_ROWS):
                 val[j : j + 1, lanes] = v[r : r + 1]
         return 0
 
@@ -430,12 +452,15 @@
     tp[0:M, :] = mm(perm, whole, NN).astype(BF)
     tp[M : 2 * M, :] = mm(perm, part, NN).astype(BF)
     state.wait()
+    ends.wait()
     puts = []
     for t in range(NT):
         at = slice(TILE * t, TILE * t + TILE)
         for kk in range(NK):
-            sp[t % 2, 8 * kk : 8 * kk + 8, :] = s_ref[kk, 0:8, at]
-            sp[t % 2, 64 + 2 * kk : 66 + 2 * kk, :] = s_ref[kk, 8:10, at]
+            sp[t % 2, 8 * kk : 8 * kk + 8, :] = s_ref[kk, :, at]
+            sp[t % 2, 64 + 2 * kk : 66 + 2 * kk, :] = s2_ref[
+                kk, 2 * (t // 2) : 2 * (t // 2) + 2, TILE * (t % 2) : TILE * (t % 2) + TILE
+            ]
         hi, lo = split(sp[t % 2])
         maps = tp[:, M * t : M * t + M]
         both = mm(maps, hi, NN)
@@ -447,11 +472,11 @@
         cp.wait()
 
 
-def window_call(g, s, mk):
+def window_call(g, s, s2, mk):
     return pl.pallas_call(
         window_kernel,
         out_shape=jax.ShapeDtypeStruct((M, CELLS), F32),
-        in_specs=[hbm(), hbm(), vm()],
+        in_specs=[hbm(), hbm(), hbm(), vm()],
         out_specs=hbm(),
         scratch_shapes=[
             pltpu.VMEM((M, WIDE), F32),
@@ -465,23 +490,25 @@
             pltpu.VMEM((640, MAPS), BF),
             pltpu.VMEM((2, M, TILE), F32),
             pltpu.VMEM((2 * M, MAPS), BF),
-            pltpu.VMEM((NC, 128, 128), F32),
-            pltpu.VMEM((NK, MLOC, CELLS), F32),
+            pltpu.VMEM((NC, ROWS, 128), F32),
+            pltpu.VMEM((NK, 8, CELLS), F32),
+            pltpu.VMEM((NK, 8, 1024), F32),
             pltpu.VMEM((M, CELLS), F32),
             pltpu.SemaphoreType.DMA((8,)),
+            pltpu.SemaphoreType.DMA(()),
             pltpu.SemaphoreType.DMA(()),
             pltpu.SemaphoreType.DMA((NT,)),
         ],
         name="window",
-    )(g, s, mk)
+    )(g, s, s2, mk)
 
 
 def local(state, obs_value, obs_var, owner, tile_of, offsets, accept, loc_mask):
     places = jnp.transpose(offsets, (0, 2, 1))
-    g, s = exchange_call(
+    g, s, s2 = exchange_call(
         owner[:, :, 0], tile_of, places, accept, obs_value, obs_var, loc_mask, state
     )
-    return window_call(g.reshape(NC, 128, 128), s, loc_mask)
+    return window_call(g.reshape(NC, ROWS, 128), s, s2, loc_mask)
 
 
 def solution(mesh):

time: 64.9 us -> 61.5 us (0.948)
  Pallas kernels: 64.6 us -> 61.2 us
    pallas_call x1, Pallas kernels: 52.2 us -> 48.7 us  [exchange_call(): pl.pallas_call(exchange_kernel, out_shape=(jax.ShapeDtypeStruct((NY, NZ,...]
where the time goes in v6:
time: 61.5 us; the launch traced here: 61.2 us
  Pallas kernels  61.2 us (100%)
    pallas_call x1, Pallas kernels, exchange_call(): pl.pallas_call(exchange_kernel, out_shape=(jax.ShapeDtypeStruct((NY, NZ,...  48.7 us
    pallas_call x1, Pallas kernels, window_call(): pl.pallas_call(window_kernel, out_shape=jax.ShapeDtypeStruct((M, CELLS),...  12.5 us

profile of v6, /device:TPU:1, one launch (start us, length us, event | category | flops | bytes accessed | tf_op | source)
XLA Modules:
  0.0 61.2 jit_solution(6527952097264200526)
XLA Ops:
  0.0 48.7 %exchange.1 = (f32[4,8,112,128]{3,2,1,0:T(8,128)}, f32[8,8,4096]{2,1,0:T(8,128)}, f32[8,8,1024]{2,1,0:T(8,128)}) custom-call(s32[4,32]{1,0:T(4,128)} %bitcast.5, s32[4,32]{1,0:T(4,128)} %ti.1, s32[4,4,32]{2,1,0:T(4,128)} %bitcast.4, s32[4,32]{1,0:T(4,128)} %ac.1, f32[4,32]{1,0:T(4,128)} %va.1, f32[4,32]{1,0:T(4,128)} %vr.1, s32[8,4,8]{2,1,0:T(4,128)} %mk_ref.1, ...), custom_call_target="tpu_custom_call" | custom-call | tf_op jit(solution)/shard_map/exchange/pallas_call | solution.py:314
  48.8 12.5 %window.1 = f32[80,4096]{1,0:T(8,128)} custom-call(f32[32,112,128]{2,1,0:T(8,128)} %bitcast.3, f32[8,8,4096]{2,1,0:T(8,128)} %get-tuple-element.9.s_hbm, f32[8,8,1024]{2,1,0:T(8,128)} %get-tuple-element.10.s2_hbm, s32[8,4,8]{2,1,0:T(4,128)} %mk_ref.1), custom_call_target="tpu_custom_call" | custom-call | tf_op jit(solution)/shard_map/window/pallas_call | solution.py:476

commit v7 on v6

--- a/solution.py
+++ b/solution.py
@@ -318,7 +318,7 @@
             jax.ShapeDtypeStruct((NK, 8, CELLS), F32),
             jax.ShapeDtypeStruct((NK, 8, 1024), F32),
         ),
-        in_specs=[vm()] * 7 + [hbm()],
+        in_specs=[vm()] * 7 + [pl.BlockSpec(memory_space=pltpu.HBM)],
         out_specs=(vm(), hbm(), hbm()),
         scratch_shapes=[
             pltpu.VMEM((MLOC, NK * CELLS), F32),
@@ -341,7 +341,7 @@
             dma((2, NY, NZ)), dma((2, NY, NZ)),
             dma((NK,)), dma((NK,)), dma((NK,)), dma((NK,)), dma(()),
         ],
-        compiler_params=pltpu.CompilerParams(collective_id=0, has_side_effects=True),
+        compiler_params=pltpu.CompilerParams(collective_id=0, has_side_effects=True, vmem_limit_bytes=52_000_000),
         name="exchange",
     )(ow, ti, of, ac, va, vr, lm, st)
 
@@ -359,19 +359,10 @@
 VALUE_ROWS = (46, 47, 54)
 
 
-def window_kernel(g_hbm, s_hbm, s2_hbm, mk_ref, out, zz, mask, val, pp, pt, dh, dl, th, tl, sp, tp, g_ref, s_ref, s2_ref, out_ref, gsem, ssem, ssem2, osem):
-    gets = [pltpu.make_async_copy(g_hbm.at[pl.ds(4 * q, 4)], g_ref.at[pl.ds(4 * q, 4)], gsem.at[q]) for q in range(8)]
-    for cp in gets:
-        cp.start()
-    state = pltpu.make_async_copy(s_hbm, s_ref, ssem)
-    state.start()
-    ends = pltpu.make_async_copy(s2_hbm, s2_ref, ssem2)
-    ends.start()
+def window_kernel(g_ref, s_ref, s2_ref, mk_ref, out, zz, mask, val, pp, pt, dh, dl, th, tl, sp, tp, out_ref, osem):
     lane_group = iota((ROWS, 128), 1) // 32
 
     def assemble(blk, _):
-        part = pl.ds(4 * blk, 4)
-        pltpu.make_async_copy(g_hbm.at[part], g_ref.at[part], gsem.at[blk]).wait()
         parts = [g_ref[4 * blk + u] for u in range(4)]
         for b in range(NB):
             v = parts[3]
@@ -451,8 +442,6 @@
     whole, part = split(zz[:, NB * 1024 :])
     tp[0:M, :] = mm(perm, whole, NN).astype(BF)
     tp[M : 2 * M, :] = mm(perm, part, NN).astype(BF)
-    state.wait()
-    ends.wait()
     puts = []
     for t in range(NT):
         at = slice(TILE * t, TILE * t + TILE)
@@ -476,7 +465,7 @@
     return pl.pallas_call(
         window_kernel,
         out_shape=jax.ShapeDtypeStruct((M, CELLS), F32),
-        in_specs=[hbm(), hbm(), hbm(), vm()],
+        in_specs=[vm()] * 4,
         out_specs=hbm(),
         scratch_shapes=[
             pltpu.VMEM((M, WIDE), F32),
@@ -490,15 +479,10 @@
             pltpu.VMEM((640, MAPS), BF),
             pltpu.VMEM((2, M, TILE), F32),
             pltpu.VMEM((2 * M, MAPS), BF),
-            pltpu.VMEM((NC, ROWS, 128), F32),
-            pltpu.VMEM((NK, 8, CELLS), F32),
-            pltpu.VMEM((NK, 8, 1024), F32),
             pltpu.VMEM((M, CELLS), F32),
-            pltpu.SemaphoreType.DMA((8,)),
-            pltpu.SemaphoreType.DMA(()),
-            pltpu.SemaphoreType.DMA(()),
             pltpu.SemaphoreType.DMA((NT,)),
         ],
+        compiler_params=pltpu.CompilerParams(vmem_limit_bytes=24 << 20),
         name="window",
     )(g, s, s2, mk)
 

time: 61.5 us -> 62.2 us (1.011)
  local copies, waits for them, and re-layouts: 0 us -> 4.82 us
  Pallas kernels: 61.2 us -> 57 us
    unnamed x0 -> x14, local copies, waits for them, and re-layouts: none -> 4.82 us
    pallas_call x1, Pallas kernels: 48.7 us -> 46.6 us  [exchange_call(): pl.pallas_call(exchange_kernel, out_shape=(jax.ShapeDtypeStruct((NY, NZ,...]
    pallas_call x1, Pallas kernels: 12.5 us -> 10.4 us  [window_call(): pl.pallas_call(window_kernel, out_shape=jax.ShapeDtypeStruct((M, CELLS),...]
where the time goes in v7:
time: 62.2 us; the launch traced here: 61.9 us
  Pallas kernels  57 us (92%)
  local copies, waits for them, and re-layouts  4.82 us (8%)
    pallas_call x1, Pallas kernels, exchange_call(): pl.pallas_call(exchange_kernel, out_shape=(jax.ShapeDtypeStruct((NY, NZ,...  46.6 us
    pallas_call x1, Pallas kernels, window_call(): pl.pallas_call(window_kernel, out_shape=jax.ShapeDtypeStruct((M, CELLS),...  10.4 us
    unnamed x14, local copies, waits for them, and re-layouts  4.82 us

profile of v7, /device:TPU:1, one launch (start us, length us, event | category | flops | bytes accessed | tf_op | source)
XLA Modules:
  0.0 61.9 jit_solution(13111691915463499499)
XLA Ops:
  0.0 0.0 copy-start
  0.0 0.7 %copy-done = s32[8,4,8]{2,1,0:T(4,128)S(1)} copy-done((s32[8,4,8]{2,1,0:T(4,128)S(1)}, s32[8,4,8]{2,1,0:T(4,128)}, u32[]{:S(2)}) %copy-start) | copy-done | bytes 1048
  0.7 0.0 copy-start.1
  0.7 0.7 %copy-done.1 = s32[4,32,4]{1,2,0:T(4,128)S(1)} copy-done((s32[4,32,4]{1,2,0:T(4,128)S(1)}, s32[4,32,4]{1,2,0:T(4,128)}, u32[]{:S(2)}) %copy-start.1) | copy-done | bytes 2072
  1.4 0.0 copy-start.2
  1.4 0.7 %copy-done.2 = s32[4,32,1]{1,2,0:T(1,128)S(1)} copy-done((s32[4,32,1]{1,2,0:T(1,128)S(1)}, s32[4,32,1]{1,2,0:T(1,128)}, u32[]{:S(2)}) %copy-start.2) | copy-done | bytes 536
  2.1 0.0 copy-start.3
  2.1 0.7 %copy-done.3 = s32[4,32]{1,0:T(4,128)S(1)} copy-done((s32[4,32]{1,0:T(4,128)S(1)}, s32[4,32]{1,0:T(4,128)}, u32[]{:S(2)}) %copy-start.3) | copy-done | bytes 536
  2.8 0.0 copy-start.4
  2.8 0.7 %copy-done.4 = s32[4,32]{1,0:T(4,128)S(1)} copy-done((s32[4,32]{1,0:T(4,128)S(1)}, s32[4,32]{1,0:T(4,128)}, u32[]{:S(2)}) %copy-start.4) | copy-done | bytes 536
  3.5 0.0 copy-start.5
  3.5 0.7 %copy-done.5 = f32[4,32]{1,0:T(4,128)S(1)} copy-done((f32[4,32]{1,0:T(4,128)S(1)}, f32[4,32]{1,0:T(4,128)}, u32[]{:S(2)}) %copy-start.5) | copy-done | bytes 536
  4.1 0.0 copy-start.6
  4.1 0.7 %copy-done.6 = f32[4,32]{1,0:T(4,128)S(1)} copy-done((f32[4,32]{1,0:T(4,128)S(1)}, f32[4,32]{1,0:T(4,128)}, u32[]{:S(2)}) %copy-start.6) | copy-done | bytes 536
  4.8 46.6 %exchange.1 = (f32[4,8,112,128]{3,2,1,0:T(8,128)S(1)}, f32[8,8,4096]{2,1,0:T(8,128)S(1)}, f32[8,8,1024]{2,1,0:T(8,128)S(1)}) custom-call(s32[4,32]{1,0:T(4,128)S(1)} %bitcast.5, s32[4,32]{1,0:T(4,128)S(1)} %copy-done.3, s32[4,4,32]{2,1,0:T(4,128)S(1)} %bitcast.4, s32[4,32]{1,0:T(4,128)S(1)} %copy-done.4, f32[4,32]{1,0:T(4,128)S(1)} %copy-done.5, ...), custom_call_target="tpu_custom_call" | custom-call | tf_op jit(solution)/shard_map/exchange/pallas_call | solution.py:314
  51.4 10.4 %window.1 = f32[80,4096]{1,0:T(8,128)} custom-call(f32[32,112,128]{2,1,0:T(8,128)S(1)} %bitcast.3, f32[8,8,4096]{2,1,0:T(8,128)S(1)} %get-tuple-element.9.s_ref, f32[8,8,1024]{2,1,0:T(8,128)S(1)} %get-tuple-element.10.s2_ref, s32[8,4,8]{2,1,0:T(4,128)S(1)} %copy-done), custom_call_target="tpu_custom_call" | custom-call | tf_op jit(solution)/shard_map/window/pallas_call | solution.py:465
Async XLA Ops:
  0.0 0.7 %copy-start = (s32[8,4,8]{2,1,0:T(4,128)S(1)}, s32[8,4,8]{2,1,0:T(4,128)}, u32[]{:S(2)}) copy-start(s32[8,4,8]{2,1,0:T(4,128)} %mk_ref.1) | copy-start | bytes 3076
  0.7 0.7 %copy-start.1 = (s32[4,32,4]{1,2,0:T(4,128)S(1)}, s32[4,32,4]{1,2,0:T(4,128)}, u32[]{:S(2)}) copy-start(s32[4,32,4]{1,2,0:T(4,128)} %param.13) | copy-start | bytes 6148
  1.4 0.7 %copy-start.2 = (s32[4,32,1]{1,2,0:T(1,128)S(1)}, s32[4,32,1]{1,2,0:T(1,128)}, u32[]{:S(2)}) copy-start(s32[4,32,1]{1,2,0:T(1,128)} %param.11) | copy-start | bytes 1540
  2.1 0.7 %copy-start.3 = (s32[4,32]{1,0:T(4,128)S(1)}, s32[4,32]{1,0:T(4,128)}, u32[]{:S(2)}) copy-start(s32[4,32]{1,0:T(4,128)} %ti.1) | copy-start | bytes 1540
  2.8 0.7 %copy-start.4 = (s32[4,32]{1,0:T(4,128)S(1)}, s32[4,32]{1,0:T(4,128)}, u32[]{:S(2)}) copy-start(s32[4,32]{1,0:T(4,128)} %ac.1) | copy-start | bytes 1540
  3.5 0.7 %copy-start.5 = (f32[4,32]{1,0:T(4,128)S(1)}, f32[4,32]{1,0:T(4,128)}, u32[]{:S(2)}) copy-start(f32[4,32]{1,0:T(4,128)} %va.1) | copy-start | bytes 1540
  4.1 0.7 %copy-start.6 = (f32[4,32]{1,0:T(4,128)S(1)}, f32[4,32]{1,0:T(4,128)}, u32[]{:S(2)}) copy-start(f32[4,32]{1,0:T(4,128)} %vr.1) | copy-start | bytes 1540

commit v8 on v7

--- a/solution.py
+++ b/solution.py
@@ -76,7 +76,8 @@
 
 
 def exchange_kernel(
-    ow, ti, of, ac, va, vr, lm, st, g_ref, s_ref, s2_ref,
+    ow_in, ti_in, of_in, ac_in, va_in, vr_in, lm_in, st, g_ref, s_ref, s2_ref,
+    ow, ti, of, ac, va, vr, lm, ins,
     stv, tiled, fi, fl, mv, mrow, rr, rsm, mks, xs, zrow, rz, blocks, tail,
     ls, own, cs, ms, mr, ks, kr, ss, rs, xss, xsr, a1s, a1r, b1s, b1r, a2s, a2r, b2s, b2r,
     pas, par, ts, tr, us, ur, own2,
@@ -92,8 +93,18 @@
         pl.semaphore_signal(bar, inc=1, device_id=(p, k), device_id_type=MESH)
     for d in FAR_K:
         pl.semaphore_signal(bar, inc=1, device_id=(c, lax.rem(k + d, NK)), device_id_type=MESH)
+    small = [
+        pltpu.make_async_copy(src, dst, ins.at[n])
+        for n, (src, dst) in enumerate(
+            ((ow_in, ow), (ti_in, ti), (of_in, of), (ac_in, ac), (va_in, va), (vr_in, vr), (lm_in, lm))
+        )
+    ]
+    for cp in small:
+        cp.start()
     load = pltpu.make_async_copy(st, stv, ls)
     load.start()
+    for cp in small:
+        cp.wait()
     mv[...] = jnp.zeros_like(mv)
     tiles = ti[...] * TILE
     cells = [tiles + of[:, p, :] for p in range(4)]
@@ -318,9 +329,17 @@
             jax.ShapeDtypeStruct((NK, 8, CELLS), F32),
             jax.ShapeDtypeStruct((NK, 8, 1024), F32),
         ),
-        in_specs=[vm()] * 7 + [pl.BlockSpec(memory_space=pltpu.HBM)],
+        in_specs=[pl.BlockSpec(memory_space=pltpu.HBM)] * 8,
         out_specs=(vm(), hbm(), hbm()),
         scratch_shapes=[
+            pltpu.VMEM((NB, 32), I32),
+            pltpu.VMEM((NB, 32), I32),
+            pltpu.VMEM((NB, 4, 32), I32),
+            pltpu.VMEM((NB, 32), I32),
+            pltpu.VMEM((NB, 32), F32),
+            pltpu.VMEM((NB, 32), F32),
+            pltpu.VMEM((NT, NB, 8), I32),
+            dma((7,)),
             pltpu.VMEM((MLOC, NK * CELLS), F32),
             pltpu.VMEM((NK * CELLS // 128, MLOC, 128), F32),
             pltpu.VMEM((8, 128), I32),
@@ -489,9 +508,8 @@
 
 def local(state, obs_value, obs_var, owner, tile_of, offsets, accept, loc_mask):
     places = jnp.transpose(offsets, (0, 2, 1))
-    g, s, s2 = exchange_call(
-        owner[:, :, 0], tile_of, places, accept, obs_value, obs_var, loc_mask, state
-    )
+    given = (owner[:, :, 0], tile_of, places, accept, obs_value, obs_var, loc_mask, state)
+    g, s, s2 = exchange_call(*(pltpu.with_memory_space_constraint(x, pltpu.HBM) for x in given))
     return window_call(g.reshape(NC, ROWS, 128), s, s2, loc_mask)
 
 

time: 62.2 us -> 57.2 us (0.920)
  local copies, waits for them, and re-layouts: 4.82 us -> 0.01 us
    unnamed x14 -> x2, local copies, waits for them, and re-layouts: 4.82 us -> 0.01 us
where the time goes in v8:
time: 57.2 us; the launch traced here: 57.1 us
  Pallas kernels  57 us (100%)
    pallas_call x1, Pallas kernels, exchange_call(): pl.pallas_call(exchange_kernel, out_shape=(jax.ShapeDtypeStruct((NY, NZ,...  46.7 us
    pallas_call x1, Pallas kernels, window_call(): pl.pallas_call(window_kernel, out_shape=jax.ShapeDtypeStruct((M, CELLS),...  10.3 us

profile of v8, /device:TPU:1, one launch (start us, length us, event | category | flops | bytes accessed | tf_op | source)
XLA Modules:
  0.0 57.1 jit_solution(6259266469643779141)
XLA Ops:
  0.0 0.0 copy-start
  0.0 46.7 %exchange.1 = (f32[4,8,112,128]{3,2,1,0:T(8,128)S(1)}, f32[8,8,4096]{2,1,0:T(8,128)S(1)}, f32[8,8,1024]{2,1,0:T(8,128)S(1)}) custom-call(s32[4,32]{1,0:T(4,128)} %bitcast.5, s32[4,32]{1,0:T(4,128)} %ti_in.1, s32[4,4,32]{2,1,0:T(4,128)} %bitcast.4, s32[4,32]{1,0:T(4,128)} %ac_in.1, f32[4,32]{1,0:T(4,128)} %va_in.1, f32[4,32]{1,0:T(4,128)} %vr_in.1, ...), custom_call_target="tpu_custom_call" | custom-call | tf_op jit(solution)/shard_map/exchange/pallas_call | solution.py:325
  46.7 0.0 copy-done
  46.8 10.3 %window.1 = f32[80,4096]{1,0:T(8,128)} custom-call(f32[32,112,128]{2,1,0:T(8,128)S(1)} %bitcast.3, f32[8,8,4096]{2,1,0:T(8,128)S(1)} %get-tuple-element.9.s_ref, f32[8,8,1024]{2,1,0:T(8,128)S(1)} %get-tuple-element.10.s2_ref, s32[8,4,8]{2,1,0:T(4,128)S(1)} %copy-done), custom_call_target="tpu_custom_call" | custom-call | tf_op jit(solution)/shard_map/window/pallas_call | solution.py:484
Async XLA Ops:
  0.0 46.7 %copy-start = (s32[8,4,8]{2,1,0:T(4,128)S(1)}, s32[8,4,8]{2,1,0:T(4,128)}, u32[]{:S(2)}) copy-start(s32[8,4,8]{2,1,0:T(4,128)} %mk_ref.1) | copy-start | bytes 3076

commit v9 on v8

--- a/solution.py
+++ b/solution.py
@@ -367,7 +367,7 @@
 
 MAPS = NT * M
 WIDE = NB * 1024 + MAPS
-CH = 512
+CH = 1024
 
 
 def mask_row(e):
@@ -404,7 +404,6 @@
     grow = jnp.where(iota((8, MAPS), 0) == iota((8, MAPS), 1) // M, 1.0, 0.0)
     for b in range(NB):
         mask[8 * b : 8 * b + 8, NB * 1024 :] = mm(mk_ref[:, b, :].astype(F32), grow, TN)
-    pp[...] = jnp.zeros_like(pp)
 
     for b in range(NB):
         lanes = slice(b * 1024, b * 1024 + 1024)
@@ -424,11 +423,11 @@
         sh, sl = split(scl)
         for q in range(8):
             w = slice(128 * q, 128 * q + 128)
-            left = jnp.concatenate([sh[:, w], sl[:, w]], axis=1)
-            right = jnp.concatenate([ih[:, w], ih[:, w]], axis=1)
-            prod = mm(left, right, NT_) + mm(sh[:, w], il[:, w], NT_)
-            pp[b % 2, 80 * q : 80 * q + 80, 0:80] = prod
-        ph, plo = split(jnp.transpose(pp[b % 2])[:M])
+            left = jnp.concatenate([ih[:, w], il[:, w]], axis=1)
+            right = jnp.concatenate([sh[:, w], sh[:, w]], axis=1)
+            prod = mm(left, right, NT_) + mm(ih[:, w], sl[:, w], NT_)
+            pp[b % 2, :, 80 * q : 80 * q + 80] = prod
+        ph, plo = split(pp[b % 2])
         pt[b, 0:M, :] = ph
         pt[b, M : 2 * M, :] = plo
 
@@ -490,7 +489,7 @@
             pltpu.VMEM((M, WIDE), F32),
             pltpu.VMEM((32, WIDE), F32),
             pltpu.VMEM((8, NB * 1024), F32),
-            pltpu.VMEM((2, 640, 128), F32),
+            pltpu.VMEM((2, M, 640), F32),
             pltpu.VMEM((NB, 2 * M, 640), BF),
             pltpu.VMEM((640, CH), BF),
             pltpu.VMEM((640, CH), BF),

time: 57.2 us -> 55.8 us (0.976)
  Pallas kernels: 57 us -> 55.7 us
    pallas_call x1, Pallas kernels: 10.3 us -> 8.95 us  [window_call(): pl.pallas_call(window_kernel, out_shape=jax.ShapeDtypeStruct((M, CELLS),...]
where the time goes in v9:
time: 55.8 us; the launch traced here: 55.7 us
  Pallas kernels  55.7 us (100%)
    pallas_call x1, Pallas kernels, exchange_call(): pl.pallas_call(exchange_kernel, out_shape=(jax.ShapeDtypeStruct((NY, NZ,...  46.7 us
    pallas_call x1, Pallas kernels, window_call(): pl.pallas_call(window_kernel, out_shape=jax.ShapeDtypeStruct((M, CELLS),...  8.95 us

profile of v9, /device:TPU:1, one launch (start us, length us, event | category | flops | bytes accessed | tf_op | source)
XLA Modules:
  0.0 55.7 jit_solution(7504970186824507470)
XLA Ops:
  0.0 0.0 copy-start
  0.0 46.7 %exchange.1 = (f32[4,8,112,128]{3,2,1,0:T(8,128)S(1)}, f32[8,8,4096]{2,1,0:T(8,128)S(1)}, f32[8,8,1024]{2,1,0:T(8,128)S(1)}) custom-call(s32[4,32]{1,0:T(4,128)} %bitcast.5, s32[4,32]{1,0:T(4,128)} %ti_in.1, s32[4,4,32]{2,1,0:T(4,128)} %bitcast.4, s32[4,32]{1,0:T(4,128)} %ac_in.1, f32[4,32]{1,0:T(4,128)} %va_in.1, f32[4,32]{1,0:T(4,128)} %vr_in.1, ...), custom_call_target="tpu_custom_call" | custom-call | tf_op jit(solution)/shard_map/exchange/pallas_call | solution.py:325
  46.7 0.0 copy-done
  46.8 8.9 %window.1 = f32[80,4096]{1,0:T(8,128)} custom-call(f32[32,112,128]{2,1,0:T(8,128)S(1)} %bitcast.3, f32[8,8,4096]{2,1,0:T(8,128)S(1)} %get-tuple-element.9.s_ref, f32[8,8,1024]{2,1,0:T(8,128)S(1)} %get-tuple-element.10.s2_ref, s32[8,4,8]{2,1,0:T(4,128)S(1)} %copy-done), custom_call_target="tpu_custom_call" | custom-call | tf_op jit(solution)/shard_map/window/pallas_call | solution.py:483
Async XLA Ops:
  0.0 46.7 %copy-start = (s32[8,4,8]{2,1,0:T(4,128)S(1)}, s32[8,4,8]{2,1,0:T(4,128)}, u32[]{:S(2)}) copy-start(s32[8,4,8]{2,1,0:T(4,128)} %mk_ref.1) | copy-start | bytes 3076

commit v10 on v9

--- a/solution.py
+++ b/solution.py
@@ -139,8 +139,6 @@
     hot = hoti.astype(F32)
     rank = jnp.sum((hoti * (seen - 1)).astype(F32), axis=0, keepdims=True)
     load.wait()
-    for t in range(NK * CELLS // 128):
-        tiled[t] = stv[:, 128 * t : 128 * t + 128]
     for p in range(NK):
         for j in range(4):
             at = CELLS * p + 1024 * j
@@ -170,6 +168,8 @@
     keep.start()
     keep2 = pltpu.make_async_copy(tail.at[k], s2_ref.at[k], own2)
     keep2.start()
+    for t in range(NK * CELLS // 128):
+        tiled[t] = stv[:, 128 * t : 128 * t + 128]
     for cp in maps:
         cp.wait()
     pick = lax.rem(c128, 16) - 10
@@ -449,7 +449,7 @@
             change(pl.ds(pl.multiple_of((b + 1) * 1024 + i * CH, CH), CH), CH, dh, dl)
             return 0
 
-        lax.fori_loop(0, (NB - 1 - b) * 1024 // CH, update, 0)
+        lax.fori_loop(0, (NB - 1 - b) * 1024 // CH, update, 0, unroll=True)
         change(slice(NB * 1024, WIDE), MAPS, th, tl)
 
     true = iota((M, M), 0)

time: 55.8 us -> 54.8 us (0.982)
  Pallas kernels: 55.7 us -> 54.6 us
    pallas_call x1, Pallas kernels: 8.95 us -> 7.91 us  [window_call(): pl.pallas_call(window_kernel, out_shape=jax.ShapeDtypeStruct((M, CELLS),...]
where the time goes in v10:
time: 54.8 us; the launch traced here: 54.7 us
  Pallas kernels  54.6 us (100%)
    pallas_call x1, Pallas kernels, exchange_call(): pl.pallas_call(exchange_kernel, out_shape=(jax.ShapeDtypeStruct((NY, NZ,...  46.7 us
    pallas_call x1, Pallas kernels, window_call(): pl.pallas_call(window_kernel, out_shape=jax.ShapeDtypeStruct((M, CELLS),...  7.91 us

profile of v10, /device:TPU:1, one launch (start us, length us, event | category | flops | bytes accessed | tf_op | source)
XLA Modules:
  0.0 54.7 jit_solution(10315540428078796836)
XLA Ops:
  0.0 0.0 copy-start
  0.0 46.7 %exchange.1 = (f32[4,8,112,128]{3,2,1,0:T(8,128)S(1)}, f32[8,8,4096]{2,1,0:T(8,128)S(1)}, f32[8,8,1024]{2,1,0:T(8,128)S(1)}) custom-call(s32[4,32]{1,0:T(4,128)} %bitcast.5, s32[4,32]{1,0:T(4,128)} %ti_in.1, s32[4,4,32]{2,1,0:T(4,128)} %bitcast.4, s32[4,32]{1,0:T(4,128)} %ac_in.1, f32[4,32]{1,0:T(4,128)} %va_in.1, f32[4,32]{1,0:T(4,128)} %vr_in.1, ...), custom_call_target="tpu_custom_call" | custom-call | tf_op jit(solution)/shard_map/exchange/pallas_call | solution.py:325
  46.7 0.0 copy-done
  46.8 7.9 %window.1 = f32[80,4096]{1,0:T(8,128)} custom-call(f32[32,112,128]{2,1,0:T(8,128)S(1)} %bitcast.3, f32[8,8,4096]{2,1,0:T(8,128)S(1)} %get-tuple-element.9.s_ref, f32[8,8,1024]{2,1,0:T(8,128)S(1)} %get-tuple-element.10.s2_ref, s32[8,4,8]{2,1,0:T(4,128)S(1)} %copy-done), custom_call_target="tpu_custom_call" | custom-call | tf_op jit(solution)/shard_map/window/pallas_call | solution.py:483
Async XLA Ops:
  0.0 46.7 %copy-start = (s32[8,4,8]{2,1,0:T(4,128)S(1)}, s32[8,4,8]{2,1,0:T(4,128)}, u32[]{:S(2)}) copy-start(s32[8,4,8]{2,1,0:T(4,128)} %mk_ref.1) | copy-start | bytes 3076
